TPU v7x, 512 devices: a whole 4x8x8 slice. The times are simulated.
512 devices in a mesh: row: 32 (over z, y_hi, core), col: 16 (over y_lo, x).
Axes of the slice: x: 4, y: 8 (y_hi: 2, y_lo: 4; y = y_hi * 4 + y_lo), z: 8, core: 2. Of those that a mesh axis runs over, the one named last changes fastest.
Arguments:
- blocks: bfloat16 [128, 192, 128, 128], P('row', 'col'), may hold values from -0.078125 to 0.078125
- columns: int32 [128, 192], P('row', 'col'), may hold values from 0 to 7
- counts: int32 [128, 16], P('row', 'col'), may hold values from 6 to 12, as said below
- inverse_diag: float32 [128, 128, 128], P('row')
- log_inverse_permeability: float32 [128, 128], P('row'), may hold values from -1 to 1
- base_velocity: float32 [128, 128], P('row'), may hold values from -6 to 6
- direction: float32 [32, 128, 128], P(None, 'row'), may hold values from -6 to 6
- obs_rows: int32 [4096], P('row'), may hold values from 0 to 3
- obs_weight: float32 [4096, 128], P('row'), may hold values from -0.5 to 0.5
- noise_prec: float32 [4096], P('row'), may hold values from 0.5 to 2
Outputs:
- hessian: float32 [32, 128, 128], P(None, 'row')
- predicted: float32 [32, 4096], P(None, 'row')
Inputs may be any that keep to these rules, and one draw needn't show every extreme that they name: `counts`: every index of row has a block row with all 12 slots live in each column group.
All inputs are finite; a program needn't handle non-finite values.
Results may differ from a plain program's by a relative error of at most 0.025.
Values may be sent and summed in bfloat16 or wider, within the bound.
No kernel may reach another device: no remote copies, remote signals or barrier semaphores. Data moves between devices by JAX's collectives and lax.ppermute only.
A program may use at most 64 MiB of HBM per device.

v0:
```python
import jax
import jax.numpy as jnp
from jax import lax
from jax.sharding import Mesh
from jax.sharding import PartitionSpec as P

COL = ("col_0", "col_1")


def broadcast(array, axis, root):
    return lax.dynamic_index_in_dim(lax.all_gather(array, axis), root, 0, keepdims=False)


def from_everyone(array, axis):
    copies = jnp.broadcast_to(array, (lax.axis_size(axis), *array.shape))
    return lax.all_to_all(copies, axis, split_axis=0, concat_axis=0, tiled=True)


def of_everyone(array, axis):
    everything = from_everyone(array, axis)
    return jnp.sum(everything, axis=0)


def split_up(array, dim, length):
    lengths = array.shape
    tiles = array.reshape(*lengths[:dim], length, lengths[dim] // length, *lengths[dim + 1 :])
    return jnp.moveaxis(tiles, dim, 0)


def sent_and_summed(array, axis, dim):
    tiles = split_up(array, dim, lax.axis_size(axis))
    arrived = lax.all_to_all(tiles, axis, split_axis=0, concat_axis=0, tiled=True)
    return arrived.astype(jnp.float32).sum(axis=0)


def from_root(array, axes, root):
    array = jnp.where(lax.axis_index(axes) == root, array, jnp.zeros_like(array))
    for axis in axes:
        array = lax.psum(array, axis)
    return array


def diag_apply(inverse_diag, values):
    return jnp.einsum("iab,sib->sia", inverse_diag, values, precision=lax.Precision.HIGHEST)


def diag_apply_t(inverse_diag, values):
    return jnp.einsum("iba,sib->sia", inverse_diag, values, precision=lax.Precision.HIGHEST)


def per_device(
    blocks,
    columns,
    counts,
    inverse_diag,
    log_inverse_permeability,
    base_velocity,
    direction,
    obs_rows,
    obs_weight,
    noise_prec,
):
    group_ratio = lax.axis_size("row") // lax.axis_size(COL)
    row_index = lax.axis_index("row")
    col_index = lax.axis_index(COL)
    nrows = blocks.shape[0]
    slot_count = blocks.shape[1]
    directions = direction.shape[0]
    trace_width = blocks.shape[2]
    group_width = nrows * group_ratio
    alpha_u = jnp.exp(log_inverse_permeability) * base_velocity
    forcing = -alpha_u[None] * direction
    live = jnp.arange(slot_count)[None, :] < counts
    flat_cols = columns.reshape(-1)
    trace_state = diag_apply(inverse_diag, forcing)
    for sweep in range(2):
        state_low = trace_state.astype(jnp.bfloat16)
        pieces = [
            broadcast(state_low, "row", col_index * group_ratio + member)
            for member in range(group_ratio)
        ]
        column_state = jnp.concatenate(pieces, axis=1)
        picked = jnp.take(column_state, flat_cols, axis=1).reshape(
            directions, nrows, slot_count, trace_width
        )
        picked = jnp.where(live[None, :, :, None], picked, jnp.zeros((), jnp.bfloat16))
        terms = jnp.einsum("ikab,sikb->sia", blocks, picked, preferred_element_type=jnp.float32)
        trace_state = diag_apply(inverse_diag, forcing - of_everyone(terms, COL))
    onehot = (obs_rows[:, None] == jnp.arange(nrows)[None, :]).astype(jnp.float32)
    sampled_draws = jnp.einsum(
        "pa,sia->spi", obs_weight, trace_state, precision=lax.Precision.HIGHEST
    )
    predicted = jnp.sum(sampled_draws * onehot[None], axis=2)
    coupling = onehot[:, :, None] * obs_weight[:, None, :]
    adjoint_force = -jnp.einsum(
        "sp,pia->sia", predicted * noise_prec[None], coupling, precision=lax.Precision.HIGHEST
    )
    targets = jax.nn.one_hot(flat_cols, group_width, dtype=jnp.float32) * live.reshape(-1)[
        :, None
    ].astype(jnp.float32)
    adjoint = diag_apply_t(inverse_diag, adjoint_force)
    for sweep in range(2):
        contrib = jnp.einsum(
            "ikab,sia->sikb",
            blocks,
            adjoint.astype(jnp.bfloat16),
            preferred_element_type=jnp.float32,
        )
        contrib = contrib.reshape(directions, nrows * slot_count, trace_width)
        column_part = jnp.einsum("snb,nj->sjb", contrib, targets, precision=lax.Precision.HIGHEST)
        column_share = sent_and_summed(column_part.astype(jnp.bfloat16), "row", 0)
        outgoing = jnp.tile(column_share, (1, lax.axis_size(COL), 1))
        owned = lax.all_to_all(
            outgoing.astype(jnp.bfloat16), "row", split_axis=1, concat_axis=0, tiled=True
        ).astype(outgoing.dtype)
        returned = from_root(owned.astype(jnp.bfloat16), COL, row_index // group_ratio).astype(
            owned.dtype
        )
        adjoint = diag_apply_t(inverse_diag, adjoint_force - returned)
    hessian = -alpha_u[None] * adjoint
    return (hessian, predicted)


def solution(mesh):
    torus = Mesh(mesh.devices.reshape(mesh.shape["row"], 4, 4), ("row", "col_0", "col_1"))
    return jax.shard_map(
        per_device,
        mesh=torus,
        in_specs=(
            P("row", COL, None, None),
            P("row", COL),
            P("row", COL),
            P("row", None, None),
            P("row", None),
            P("row", None),
            P(None, "row", None),
            P("row"),
            P("row", None),
            P("row"),
        ),
        out_specs=(P(None, "row", None), P(None, "row")),
        check_vma=False,
    )
```

profile of v0, /device:TPU:1, one launch (start us, length us, event | category | flops | bytes accessed | tf_op | source)
XLA Modules:
  0.0 385.4 jit_solution(14018968457608506230)
XLA Ops:
  7.2 0.8 multiply_negate_fusion
  8.0 2.1 fusion.5
  10.3 0.8 reshape.169
  11.0 0.7 fusion.48
  11.8 86.5 %all-gather.5.cloned.1.call-done = bf16[1024,4,128]{2,0,1:T(8,128)(2,1)} async-done(((bf16[32,4,128]{2,0,1:T(8,128)(2,1)}), bf16[1024,4,128]{2,0,1:T(8,128)(2,1)}) %all-gather.5.cloned.1.call-update) | async-done | bytes 1048592 | tf_op jit(solution)/shard_map/all_gather | solution.py:11
  98.2 0.8 dynamic-slice_bitcast_fusion.3
  99.0 0.6 gather_fusion
  99.7 0.1 broadcast_select_fusion
  99.8 0.6 convolution_bitcast_fusion.3
  100.5 0.1 broadcast_in_dim.46
  100.6 31.6 %all_to_all.38 = f32[16,32,4,128]{3,1,2,0:T(8,128)S(1)} all-to-all(f32[16,32,4,128]{3,1,2,0:T(8,128)S(1)} %broadcast_in_dim.46), channel_id=1, replica_groups=mesh['row'=32,'col_0'=4,'col_1'=4] {'col_0','col_1'}, dimensions={0} | all-to-all | bytes 2097152 | tf_op jit(solution)/shard_map/all_to_all | solution.py:16
  132.3 0.1 reduce_sum.51
  132.4 1.1 fusion.6
  133.5 77.2 %all-gather.7.cloned.1.call-done = bf16[1024,4,128]{2,0,1:T(8,128)(2,1)} async-done(((bf16[32,4,128]{2,0,1:T(8,128)(2,1)}), bf16[1024,4,128]{2,0,1:T(8,128)(2,1)}) %all-gather.7.cloned.1.call-update) | async-done | bytes 1048592 | tf_op jit(solution)/shard_map/all_gather | solution.py:11
  210.7 0.8 dynamic-slice_bitcast_fusion.1
  211.5 0.6 gather_fusion.1
  212.2 0.1 broadcast_select_fusion.1
  212.3 0.6 convolution_bitcast_fusion.2
  212.9 1.1 broadcast_in_dim.47
  214.1 7.0 %all-to-all-start.1 = ((f32[16,32,4,128]{3,1,2,0:T(8,128)}), f32[16,32,4,128]{3,1,2,0:T(8,128)S(1)}, u32[]{:S(2)}, u32[]{:S(2)}) async-start(f32[16,32,4,128]{3,1,2,0:T(8,128)} %broadcast_in_dim.47), calls=%async_computation.1 | async-start | bytes 2097152 | tf_op jit(solution)/shard_map/all_to_all | solution.py:16
  221.0 0.1 reshape.176
  221.1 22.7 %all-to-all-done.1 = f32[16,32,4,128]{3,1,2,0:T(8,128)S(1)} async-done(((f32[16,32,4,128]{3,1,2,0:T(8,128)}), f32[16,32,4,128]{3,1,2,0:T(8,128)S(1)}, u32[]{:S(2)}, u32[]{:S(2)}) %all-to-all-start.1) | async-done | bytes 1048608 | tf_op jit(solution)/shard_map/all_to_all | solution.py:16
  243.8 0.1 reduce_sum.52
  243.9 0.5 convolution_bitcast_fusion.1
  244.4 0.3 fusion.4
  244.7 0.4 convolution_negate_fusion
  245.0 0.3 fusion.7
  245.4 0.3 fusion.49
  245.7 0.9 fusion
  246.6 20.8 %all_to_all.39 = bf16[32,1,8,128]{3,2,1,0:T(8,128)(2,1)S(1)} all-to-all(bf16[32,1,8,128]{3,2,1,0:T(8,128)(2,1)S(1)} %fusion), channel_id=1, replica_groups=mesh['row'=32,'col_0'=4,'col_1'=4] {'row'}, dimensions={0} | all-to-all | bytes 131072 | tf_op jit(solution)/shard_map/all_to_all | solution.py:32
  267.5 0.1 copy.91
  267.6 0.6 broadcast.101
  268.2 0.9 reduce.4
  269.0 0.6 reshape.208
  269.7 3.9 %all-to-all-start.3 = ((bf16[32,2,256]{2,1,0:T(2,128)(2,1)}), bf16[32,2,256]{2,1,0:T(2,128)(2,1)S(1)}, u32[]{:S(2)}, u32[]{:S(2)}) async-start(bf16[32,2,256]{2,1,0:T(2,128)(2,1)} %reshape.208), calls=%async_computation.3 | async-start | bytes 65536 | tf_op jit(solution)/shard_map/all_to_all | solution.py:113
  273.6 12.1 %all-to-all-done.3 = bf16[32,2,256]{2,1,0:T(2,128)(2,1)S(1)} async-done(((bf16[32,2,256]{2,1,0:T(2,128)(2,1)}), bf16[32,2,256]{2,1,0:T(2,128)(2,1)S(1)}, u32[]{:S(2)}, u32[]{:S(2)}) %all-to-all-start.3) | async-done | bytes 32800 | tf_op jit(solution)/shard_map/all_to_all | solution.py:113
  285.8 15.1 %psum.28 = bf16[32,4,128]{2,0,1:T(8,128)(2,1)S(1)} all-reduce(bf16[32,4,128]{2,0,1:T(8,128)(2,1)S(1)} %copy.63), channel_id=1, replica_groups=mesh['row'=32,'col_0'=4,'col_1'=4] {'col_0'}, use_global_device_ids=true, to_apply=%region_4.6 | all-reduce | flops 16384 | bytes 65536 | tf_op jit(solution)/shard_map/psum | solution.py:39
  301.0 12.8 %psum.29 = bf16[32,4,128]{2,0,1:T(8,128)(2,1)S(1)} all-reduce(bf16[32,4,128]{2,0,1:T(8,128)(2,1)S(1)} %psum.28), channel_id=1, replica_groups=mesh['row'=32,'col_0'=4,'col_1'=4] {'col_1'}, use_global_device_ids=true, to_apply=%region_5.7 | all-reduce | flops 16384 | bytes 65536 | tf_op jit(solution)/shard_map/psum | solution.py:39
  313.7 0.3 fusion.8
  314.1 0.3 fusion.50
  314.4 0.9 fusion.1
  315.3 22.6 %all_to_all.40 = bf16[32,1,8,128]{3,2,1,0:T(8,128)(2,1)S(1)} all-to-all(bf16[32,1,8,128]{3,2,1,0:T(8,128)(2,1)S(1)} %fusion.1), channel_id=1, replica_groups=mesh['row'=32,'col_0'=4,'col_1'=4] {'row'}, dimensions={0} | all-to-all | bytes 131072 | tf_op jit(solution)/shard_map/all_to_all | solution.py:32
  338.0 0.9 reduce.5
  338.9 15.2 %all_to_all.41 = bf16[32,2,256]{2,1,0:T(2,128)(2,1)S(1)} all-to-all(bf16[32,2,256]{2,1,0:T(2,128)(2,1)S(1)} %reshape.210), channel_id=1, replica_groups=mesh['row'=32,'col_0'=4,'col_1'=4] {'row'}, dimensions={0} | all-to-all | bytes 65536 | tf_op jit(solution)/shard_map/all_to_all | solution.py:113
  354.1 12.4 %psum.30 = bf16[32,4,128]{2,0,1:T(8,128)(2,1)S(1)} all-reduce(bf16[32,4,128]{2,0,1:T(8,128)(2,1)S(1)} %copy.68), channel_id=1, replica_groups=mesh['row'=32,'col_0'=4,'col_1'=4] {'col_0'}, use_global_device_ids=true, to_apply=%region_7.9 | all-reduce | flops 16384 | bytes 65536 | tf_op jit(solution)/shard_map/psum | solution.py:39
  366.6 11.0 %psum.31 = bf16[32,4,128]{2,0,1:T(8,128)(2,1)S(1)} all-reduce(bf16[32,4,128]{2,0,1:T(8,128)(2,1)S(1)} %psum.30), channel_id=1, replica_groups=mesh['row'=32,'col_0'=4,'col_1'=4] {'col_1'}, use_global_device_ids=true, to_apply=%region_8.10 | all-reduce | flops 16384 | bytes 65536 | tf_op jit(solution)/shard_map/psum | solution.py:39
  377.5 0.3 fusion.3
  377.9 0.7 copy.69
  (36 shorter events, 0.5 us)
Async XLA Ops:
  7.2 92.6 %copy-start = (bf16[4,12,128,128]{3,2,1,0:T(8,128)(2,1)S(1)}, bf16[4,12,128,128]{3,2,1,0:T(8,128)(2,1)}, u32[]{:S(2)}) copy-start(bf16[4,12,128,128]{3,2,1,0:T(8,128)(2,1)} %param.12) | copy-start | bytes 4718596
  7.2 91.1 %all-gather.5.cloned.1.call-start = ((), (), s32[]{:S(2)}) async-start(), calls=%async_computation.6 | async-start | bytes 1081344 | tf_op jit(solution)/shard_map/all_gather | solution.py:11
  10.2 200.5 %all-gather.7.cloned.1.call-start = ((), (), s32[]{:S(2)}) async-start(), calls=%async_computation.7 | async-start | bytes 1081344 | tf_op jit(solution)/shard_map/all_gather | solution.py:11
  100.6 31.7 %copy-start.1 = (f32[4,128,128]{2,1,0:T(8,128)S(1)}, f32[4,128,128]{2,1,0:T(8,128)}, u32[]{:S(2)}) copy-start(f32[4,128,128]{2,1,0:T(8,128)} %param.15) | copy-start | bytes 786436
  100.6 31.7 %copy-start.2 = (f32[32,4,128]{2,1,0:T(4,128)S(1)}, f32[32,4,128]{2,1,0:T(4,128)}, u32[]{:S(2)}) copy-start(f32[32,4,128]{2,1,0:T(4,128)} %param.18) | copy-start | bytes 196612
  212.9 8.2 %copy-start.6 = (s32[128]{0:T(128)S(1)}, s32[128]{0:T(128)}, u32[]{:S(2)}) copy-start(s32[128]{0:T(128)} %param.19) | copy-start | bytes 1540
  214.1 30.3 %copy-start.3 = (f32[128,128]{1,0:T(8,128)S(1)}, f32[128,128]{1,0:T(8,128)}, u32[]{:S(2)}) copy-start(f32[128,128]{1,0:T(8,128)} %param.20) | copy-start | bytes 196612
  214.1 30.6 %copy-start.5 = (f32[128]{0:T(128)S(1)}, f32[128]{0:T(128)}, u32[]{:S(2)}) copy-start(f32[128]{0:T(128)} %param.21) | copy-start | bytes 1540
  214.1 29.7 %all-to-all-start.1 = ((f32[16,32,4,128]{3,1,2,0:T(8,128)}), f32[16,32,4,128]{3,1,2,0:T(8,128)S(1)}, u32[]{:S(2)}, u32[]{:S(2)}) async-start(f32[16,32,4,128]{3,1,2,0:T(8,128)} %broadcast_in_dim.47), calls=%async_computation.1 | async-start | bytes 2097152 | tf_op jit(solution)/shard_map/all_to_all | solution.py:16
  244.7 2.0 copy-start.4
  269.7 16.1 %all-to-all-start.3 = ((bf16[32,2,256]{2,1,0:T(2,128)(2,1)}), bf16[32,2,256]{2,1,0:T(2,128)(2,1)S(1)}, u32[]{:S(2)}, u32[]{:S(2)}) async-start(bf16[32,2,256]{2,1,0:T(2,128)(2,1)} %reshape.208), calls=%async_computation.3 | async-start | bytes 65536 | tf_op jit(solution)/shard_map/all_to_all | solution.py:113
Sparse Core Ops, SparseCore 0:
  11.7 86.5 all-gather.4
  133.6 77.0 all-gather.6
where the time goes:
time: 391 us; the launch traced here: 385 us
  waiting for transfers between devices  198 us (51%)
  blocking collectives  141 us (36%)
  between operations  14.3 us (4%)
  starting transfers between devices  11 us (3%)
  matrix products  9.23 us (2%)
  local copies, waits for them, and re-layouts  7.09 us (2%)
    all_gather x2, waiting for transfers between devices, broadcast(): lax.all_gather(array, axis)  164 us
    psum x4, blocking collectives, from_root(): array = lax.psum(array, axis)  51.3 us
    all_to_all x2, blocking collectives, sent_and_summed(): lax.all_to_all(tiles, axis, split_axis=0, concat_axis=0, tiled=True)  43.4 us
    all_to_all x1, blocking collectives, from_everyone(): return lax.all_to_all(copies, axis, split_axis=0, concat_axis=0, tiled=True)  31.6 us
    all_to_all x1, waiting for transfers between devices, from_everyone(): return lax.all_to_all(copies, axis, split_axis=0, concat_axis=0, tiled=True)  22.7 us
    all_to_all x1, blocking collectives, per_device(): lax.all_to_all(outgoing.astype(jnp.bfloat16), 'row', split_axis=1, concat...  15.2 us
    all_to_all x1, waiting for transfers between devices, per_device(): lax.all_to_all(outgoing.astype(jnp.bfloat16), 'row', split_axis=1, concat...  12.1 us
  transfers between devices with their start and end apart: 4, of which 4 were waited for; matrix products, arithmetic and copies ran while one was open for 0% of the time, Pallas kernels for 0%

commit v1 on v0

v1 whole, which is shorter than its diff:
```python
import jax
import jax.numpy as jnp
from jax import lax
from jax.experimental import pallas as pl
from jax.experimental.pallas import tpu as pltpu
from jax.sharding import Mesh
from jax.sharding import PartitionSpec as P

AXES = ("zh", "z0", "h", "k", "l", "x")
SIZES = (4, 2, 2, 2, 4, 4)
ROW = ("zh", "z0", "h", "k")
COL = ("l", "x")
NEAR = ("z0", "h", "l", "x")
FAR = ("zh", "z0", "h", "l")
F32 = jnp.float32
BF16 = jnp.bfloat16
HIGHEST = lax.Precision.HIGHEST
VMEM = pl.BlockSpec(memory_space=pltpu.VMEM)
SMEM = pl.BlockSpec(memory_space=pltpu.SMEM)

ZH, CROSS, CORE, LCOL, XCOL = range(5)


def matmul(a, b, precision=None):
    return lax.dot_general(a, b, (((1,), (0,)), ((), ())), precision=precision, preferred_element_type=F32)


def matmul_t(a, b, precision=None):
    return lax.dot_general(a, b, (((1,), (1,)), ((), ())), precision=precision, preferred_element_type=F32)


def call(kernel, outs, scalars, arrays, scratch=(), cost=None):
    return pl.pallas_call(
        kernel,
        out_shape=[jax.ShapeDtypeStruct(shape, dtype) for shape, dtype in outs],
        in_specs=[SMEM] * len(scalars) + [VMEM] * len(arrays),
        out_specs=[VMEM] * len(outs),
        scratch_shapes=list(scratch),
        cost_estimate=cost,
    )(*scalars, *arrays)


def first_state(inverse_ref, log_ref, base_ref, direction_ref, weight_ref, onehot_ref, g_ref, low_ref, seen_ref):
    alpha_u = jnp.exp(log_ref[...]) * base_ref[...]
    seen = jnp.zeros(seen_ref.shape, F32)
    weight = weight_ref[...]
    for q in range(4):
        forcing = -alpha_u[q][None, :] * direction_ref[:, q, :]
        state = matmul_t(forcing, inverse_ref[q], HIGHEST)
        g_ref[:, q * 128 : (q + 1) * 128] = state
        low_ref[:, q * 128 : (q + 1) * 128] = state.astype(BF16)
        seen += matmul_t(state, weight, HIGHEST) * onehot_ref[q][None, :]
    seen_ref[...] = seen


def build(columns_ref, counts_ref, blocks_ref, inverse_ref, weight_ref, onehot_ref, out_ref, dense):
    for q in range(4):
        dense[...] = jnp.zeros(dense.shape, F32)

        def add(slot, carry):
            column = columns_ref[q, slot]
            dense[column] += blocks_ref[q, slot].astype(F32)
            return carry

        lax.fori_loop(0, counts_ref[q, 0], add, 0)
        for c in range(8):
            out_ref[q * 128 : (q + 1) * 128, c * 128 : (c + 1) * 128] = matmul(
                inverse_ref[q], dense[c], HIGHEST
            ).astype(BF16)
    observed = jnp.zeros((128, 1024), F32)
    for q in range(4):
        coupling = (weight_ref[...] * onehot_ref[:, q : q + 1]).astype(BF16)
        observed += matmul(coupling, out_ref[q * 128 : (q + 1) * 128, :])
        rows = 640 + 32 * q
        for part in range(4):
            out_ref[640 + part * 32 : 672 + part * 32, q * 128 : (q + 1) * 128] = coupling[part * 32 : part * 32 + 32]
    out_ref[512:640, :] = observed.astype(BF16)
    out_ref[640:768, 512:1024] = jnp.zeros((128, 512), BF16)


def put_tiles(out_ref, values, first_block, near):
    for q in range(values.shape[1] // 128):
        for half in range(2):
            tile = values[half * 8 : half * 8 + 8, q * 128 : (q + 1) * 128].astype(BF16)
            share = (first_block + q) * 2 + half
            for copy in range(4):
                out_ref[share * 4 + copy if near else copy * 16 + share] = tile


def forward_one(at_ref, first_ref, second_ref, own_ref, other_ref, g_ref, g_other_ref, out_ref, state):
    core = at_ref[CORE]
    mine, theirs = core * 4, (1 - core) * 4
    state[:, pl.ds(pl.multiple_of(core * 512, 512), 512)] = first_ref[...]
    state[:, pl.ds(pl.multiple_of((1 - core) * 512, 512), 512)] = second_ref[...]
    low = state[...]
    put_tiles(out_ref, g_ref[...] * (1.0 / 16) - matmul_t(low, own_ref[0:512, :]), mine, True)
    put_tiles(out_ref, g_other_ref[...] * (1.0 / 16) - matmul_t(low, other_ref[0:512, :]), theirs, True)


def sum_near(at_ref, in_ref, out_ref):
    first = at_ref[XCOL] * 16
    total = in_ref[first].astype(F32)
    for source in range(1, 16):
        total += in_ref[first + source].astype(F32)
    out_ref[...] = jnp.broadcast_to(total.astype(BF16)[None], out_ref.shape)


def sum_far(at_ref, in_ref, out_ref):
    first = at_ref[ZH]
    total = in_ref[first].astype(F32)
    for source in range(1, 16):
        total += in_ref[first + 4 * source].astype(F32)
    out_ref[...] = jnp.broadcast_to(total.astype(BF16)[None], out_ref.shape)


def forward_two(at_ref, in_ref, own_ref, other_ref, seen_ref, seen_other_ref, out_ref, state):
    first = at_ref[LCOL] * 16
    for block in range(8):
        for half in range(2):
            state[half * 8 : half * 8 + 8, block * 128 : (block + 1) * 128] = in_ref[first + block * 2 + half].astype(F32)
    low = state[...].astype(BF16)
    mine = seen_ref[...] * (1.0 / 16) - matmul_t(low, own_ref[512:640, :])
    theirs = seen_other_ref[...] * (1.0 / 16) - matmul_t(low, other_ref[512:640, :])
    for copy in range(16):
        out_ref[copy, :, 0:128] = mine.astype(BF16)
        out_ref[copy, :, 128:256] = theirs.astype(BF16)


def adjoint_one(at_ref, in_ref, own_ref, other_ref, noise_ref, noise_other_ref, out_ref, mine_ref, theirs_ref, force_ref):
    core = at_ref[CORE]
    predicted = in_ref[0].astype(F32)
    for source in range(1, 16):
        predicted += in_ref[source].astype(F32)
    mine_ref[...] = predicted[:, 0:128]
    theirs_ref[...] = predicted[:, 128:256]
    scaled = (predicted[:, 0:128] * noise_ref[...]).astype(BF16)
    scaled_other = (predicted[:, 128:256] * noise_other_ref[...]).astype(BF16)
    put_tiles(out_ref, matmul(scaled, own_ref[512:640, :]) + matmul(scaled_other, other_ref[512:640, :]), 0, False)
    force_ref[:, 0:512] = -matmul(scaled, own_ref[640:768, 0:512])
    force_ref[:, 512:1024] = -matmul(scaled_other, other_ref[640:768, 0:512])


def gather_rows(at_ref, in_ref, force_ref, state):
    core, cross = at_ref[CORE], at_ref[CROSS]
    for side in range(2):
        first_block = (core if side == 0 else 1 - core) * 4
        for q in range(4):
            lanes = slice(side * 512 + q * 128, side * 512 + (q + 1) * 128)
            for half in range(2):
                share = (first_block + q) * 2 + half
                state[half * 8 : half * 8 + 8, lanes] = (
                    force_ref[half * 8 : half * 8 + 8, lanes] + in_ref[share * 4 + cross].astype(F32)
                )


def adjoint_two(at_ref, in_ref, own_ref, other_ref, force_ref, out_ref, state):
    gather_rows(at_ref, in_ref, force_ref, state)
    low = state[...].astype(BF16)
    total = matmul(low[:, 0:512], own_ref[0:512, :]) + matmul(low[:, 512:1024], other_ref[0:512, :])
    put_tiles(out_ref, -total, 0, False)


def adjoint_end(at_ref, in_ref, force_ref, mine_ref, theirs_ref, state):
    gather_rows(at_ref, in_ref, force_ref, state)
    mine_ref[...] = state[:, 0:512]
    theirs_ref[...] = state[:, 512:1024]


def finish(at_ref, mine_ref, theirs_ref, inverse_ref, log_ref, base_ref, out_ref):
    alpha_u = jnp.exp(log_ref[...]) * base_ref[...]
    core = at_ref[CORE]
    for part, ref in ((core, mine_ref), (1 - core, theirs_ref)):
        for q in range(4):
            adjoint = matmul(ref[:, q * 128 : (q + 1) * 128], inverse_ref[q], HIGHEST)
            out_ref[pl.ds(part * 16, 16), q, :] = -alpha_u[q][None, :] * adjoint


def transposed(flip):
    pairs = []
    for zh in range(4):
        for cross in range(4):
            for k in range(2):
                for l in range(4):
                    for x in range(4):
                        source = (((zh * 4 + cross) * 2 + k) * 4 + l) * 4 + x
                        target = (((l * 4 + x) * 2 + (k ^ flip)) * 4 + zh) * 4 + cross
                        pairs.append((source, target))
    return pairs


def swapped(array):
    return lax.ppermute(array, "k", [(0, 1), (1, 0)])


def exchange(array, axes):
    return lax.all_to_all(array, axes, split_axis=0, concat_axis=0, tiled=True)


def per_device(
    blocks, columns, counts, inverse_diag, log_inverse_permeability, base_velocity, direction, obs_rows, obs_weight, noise_prec
):
    zh, z0, h, k, l, x = (lax.axis_index(axis) for axis in AXES)
    at = jnp.stack([zh, z0 * 2 + h, k, l, x]).astype(jnp.int32)
    onehot = (obs_rows[None, :] == jnp.arange(4)[:, None]).astype(F32)
    onehot_t = (obs_rows[:, None] == jnp.arange(4)[None, :]).astype(F32)

    g, low, seen = call(
        first_state,
        [((32, 512), F32), ((32, 512), BF16), ((32, 128), F32)],
        [],
        [inverse_diag, log_inverse_permeability, base_velocity, direction, obs_weight, onehot],
    )

    def half(array, which):
        return lax.dynamic_slice_in_dim(array, which * 16, 16, 0)

    first = lax.ppermute(half(low, k), AXES, transposed(0))
    second = lax.ppermute(half(low, 1 - k), AXES, transposed(1))
    sent = jnp.concatenate([half(g, 1 - k), half(seen, 1 - k), jnp.broadcast_to(noise_prec[None, :], (16, 128))], axis=1)
    came = swapped(sent)
    g_mine, g_other = half(g, k), came[:, 0:512]
    seen_mine, seen_other = half(seen, k), came[:, 512:640]
    noise, noise_other = noise_prec[None, :], came[0:1, 640:768]

    (own,) = call(
        build,
        [((768, 1024), BF16)],
        [columns, counts],
        [blocks, inverse_diag, obs_weight, onehot_t],
        [pltpu.VMEM((8, 128, 128), F32)],
        pl.CostEstimate(flops=2 * 10**9, bytes_accessed=4 * 10**6, transcendentals=0),
    )
    other = swapped(own)

    tiles = ((64, 8, 128), BF16)
    low_state = [pltpu.VMEM((16, 1024), BF16)]
    full_state = [pltpu.VMEM((16, 1024), F32)]
    (part,) = call(forward_one, [tiles], [at], [first, second, own, other, g_mine, g_other], low_state)
    (part,) = call(sum_near, [tiles], [at], [exchange(part, NEAR)])
    (part,) = call(
        forward_two, [((16, 16, 256), BF16)], [at], [exchange(part, FAR), own, other, seen_mine, seen_other], full_state
    )
    part, predicted, predicted_other, force = call(
        adjoint_one,
        [tiles, ((16, 128), F32), ((16, 128), F32), ((16, 1024), F32)],
        [at],
        [exchange(part, COL), own, other, noise, noise_other],
    )
    predicted_came = swapped(predicted_other)
    (part,) = call(sum_far, [tiles], [at], [exchange(part, FAR)])
    (part,) = call(adjoint_two, [tiles], [at], [exchange(part, NEAR), own, other, force], full_state)
    (part,) = call(sum_far, [tiles], [at], [exchange(part, FAR)])
    mine, theirs = call(
        adjoint_end, [((16, 512), F32), ((16, 512), F32)], [at], [exchange(part, NEAR), force], full_state
    )
    (hessian,) = call(
        finish,
        [((32, 4, 128), F32)],
        [at],
        [mine, swapped(theirs), inverse_diag, log_inverse_permeability, base_velocity],
    )
    both = jnp.where(k == 0, jnp.stack([predicted, predicted_came]), jnp.stack([predicted_came, predicted]))
    return (hessian, both.reshape(32, 128))


def solution(mesh):
    grid = Mesh(mesh.devices.reshape(SIZES), AXES)
    return jax.shard_map(
        per_device,
        mesh=grid,
        in_specs=(
            P(ROW, COL, None, None),
            P(ROW, COL),
            P(ROW, COL),
            P(ROW, None, None),
            P(ROW, None),
            P(ROW, None),
            P(None, ROW, None),
            P(ROW),
            P(ROW, None),
            P(ROW),
        ),
        out_specs=(P(None, ROW, None), P(None, ROW)),
        check_vma=False,
    )
```

time: 391 us -> 196 us (0.50); the launches traced: 385 us -> 195 us
  waiting for transfers between devices: 198 us -> 19.6 us
  blocking collectives: 141 us -> 84.9 us
  starting transfers between devices: 11 us -> 46.7 us
  Pallas kernels: 0 us -> 29.1 us
  between operations: 14.3 us -> 0.82 us
  matrix products: 9.23 us -> 0 us
    all_gather x2 -> x0, waiting for transfers between devices: 164 us -> none  [broadcast(): lax.all_gather(array, axis)]
    psum x4 -> x0, blocking collectives: 51.3 us -> none  [from_root(): array = lax.psum(array, axis)]
    ppermute x0 -> x6, starting transfers between devices: none -> 32.8 us  [the longest x4 29.7 us: swapped(): return lax.ppermute(array, 'k', [(0, 1), (1, 0)])]
    pallas_call x0 -> x11, Pallas kernels: none -> 29.1 us  [call(): pl.pallas_call(kernel, out_shape=[jax.ShapeDtypeStruct(shape, dtype) for...]
    all_to_all x2 -> x3, waiting for transfers between devices: 34.8 us -> 19.2 us  [exchange(): return lax.all_to_all(array, axes, split_axis=0, concat_axis=0, tiled=True)]
    dot_general x14 -> x0, matrix products: 9.23 us -> none  [the longest x3 3.79 us: diag_apply(): jnp.einsum('iab,sib->sia', inverse_diag, values, precision=lax.Precision....]
    all_to_all x4, blocking collectives: 90.2 us -> 84.9 us  [exchange(): return lax.all_to_all(array, axes, split_axis=0, concat_axis=0, tiled=True)]
    all_to_all x2 -> x3, starting transfers between devices: 10.9 us -> 13.9 us  [exchange(): return lax.all_to_all(array, axes, split_axis=0, concat_axis=0, tiled=True)]
  transfers between devices with their start and end apart: 4 -> 9, of which waited for: 4 -> 4; matrix products, arithmetic and copies ran while one was open for 0% -> 4% of each run, Pallas kernels for 0% -> 2%
where the time goes in v1:
time: 196 us; the launch traced here: 195 us
  blocking collectives  84.9 us (43%)
  starting transfers between devices  46.7 us (24%)
  Pallas kernels  29.1 us (15%)
  waiting for transfers between devices  19.6 us (10%)
  local copies, waits for them, and re-layouts  10.8 us (6%)
  other arithmetic  2.58 us (1%)
    all_to_all x4, blocking collectives, exchange(): return lax.all_to_all(array, axes, split_axis=0, concat_axis=0, tiled=True)  84.9 us
    ppermute x4, starting transfers between devices, swapped(): return lax.ppermute(array, 'k', [(0, 1), (1, 0)])  29.7 us
    pallas_call x11, Pallas kernels, call(): pl.pallas_call(kernel, out_shape=[jax.ShapeDtypeStruct(shape, dtype) for...  29.1 us
    all_to_all x3, waiting for transfers between devices, exchange(): return lax.all_to_all(array, axes, split_axis=0, concat_axis=0, tiled=True)  19.2 us
    all_to_all x3, starting transfers between devices, exchange(): return lax.all_to_all(array, axes, split_axis=0, concat_axis=0, tiled=True)  13.9 us
    unnamed x23, local copies, waits for them, and re-layouts  5.05 us
  transfers between devices with their start and end apart: 9, of which 4 were waited for; matrix products, arithmetic and copies ran while one was open for 4% of the time, Pallas kernels for 2%

profile of v1, /device:TPU:1, one launch (start us, length us, event | category | flops | bytes accessed | tf_op | source)
XLA Modules:
  0.0 194.6 jit_solution(18104625782411394016)
XLA Ops:
  0.6 1.4 fusion.onehot_ref
  2.0 1.3 copy.12.counts_ref
  3.3 5.8 %shard_map.114.own_ref = bf16[768,1024]{1,0:T(8,128)(2,1)} custom-call(s32[4,12]{1,0:T(4,128)} %columns_ref.1, s32[4,1]{1,0:T(4,128)} %copy.12.counts_ref, bf16[4,12,128,128]{3,2,1,0:T(8,128)(2,1)} %blocks_ref.1, f32[4,128,128]{2,1,0:T(8,128)} %inverse_ref.5, f32[128,128]{1,0:T(8,128)} %weight_ref.3, f32[128,4]{1,0:T(8,128)} %fusion.onehot_ref), custom_call_target="tpu_custom_call" | custom-call | flops 2000000000 | bytes 4000000 | tf_op jit(solution)/shard_map/pallas_call | solution.py:33
  9.1 8.7 %collective-permute-start.2 = (bf16[768,1024]{1,0:T(8,128)(2,1)}, bf16[768,1024]{1,0:T(8,128)(2,1)S(1)}, u32[]{:S(2)}, u32[]{:S(2)}) collective-permute-start(bf16[768,1024]{1,0:T(8,128)(2,1)} %shard_map.114.own_ref), channel_id=1, source_target_pairs={{0,16},{16,0},{1,17},{17,1},{2,18},{18,2},{3,19},{19,3},{4,20},{20... | collective-permute-start | bytes 4718600 | tf_op jit(solution)/shard_map/ppermute | solution.py:192
  17.8 0.6 fusion.1.onehot_ref
  18.4 2.8 %shard_map.113 = (f32[32,512]{1,0:T(8,128)}, bf16[32,512]{1,0:T(8,128)(2,1)}, f32[32,128]{1,0:T(8,128)}) custom-call(f32[4,128,128]{2,1,0:T(8,128)} %inverse_ref.5, f32[4,128]{1,0:T(4,128)} %log_ref.3, f32[4,128]{1,0:T(4,128)} %base_ref.3, f32[32,4,128]{2,1,0:T(4,128)} %direction_ref.1, f32[128,128]{1,0:T(8,128)} %weight_ref.3, f32[4,128]{1,0:T(4,128)} %fusion.1.onehot_ref), custom_call_target="tpu_custom_call" | custom-call | tf_op jit(solution)/shard_map/pallas_call | solution.py:33
  21.2 1.3 constant_dynamic-slice_fusion
  22.6 1.4 constant_dynamic-slice_fusion.2
  24.0 1.9 collective-permute-start.3
  25.9 0.7 constant_dynamic-slice_fusion.4
  26.6 0.7 collective-permute-start
  27.3 2.4 %collective-permute-start.1 = (bf16[16,512]{1,0:T(8,128)(2,1)S(1)}, bf16[16,512]{1,0:T(8,128)(2,1)S(1)}, u32[]{:S(2)}, u32[]{:S(2)}) collective-permute-start(bf16[16,512]{1,0:T(8,128)(2,1)S(1)} %get-tuple-element.22), channel_id=1, source_target_pairs={{0,16},{1,48},{2,80},{3,112},{4,144},{5,176},{6,208},{7,240},{8,27... | collective-permute-start | bytes 49160 | tf_op jit(solution)/shard_map/ppermute | solution.py:218
  29.7 0.7 stack.37.at_ref
  30.4 0.0 collective-permute-done.3
  30.4 0.6 slice.12.g_other_ref
  31.0 0.0 collective-permute-done.first_ref
  31.0 0.0 collective-permute-done.1.second_ref
  31.0 0.6 copy-done.5
  31.6 0.6 copy-done
  32.2 3.2 %shard_map.115 = bf16[64,8,128]{2,1,0:T(8,128)(2,1)} custom-call(s32[5]{0:T(128)} %stack.37.at_ref, bf16[16,512]{1,0:T(8,128)(2,1)} %copy-done.5, bf16[16,512]{1,0:T(8,128)(2,1)} %copy-done.6, bf16[768,1024]{1,0:T(8,128)(2,1)} %shard_map.114.own_ref, bf16[768,1024]{1,0:T(8,128)(2,1)} %copy-done, f32[16,512]{1,0:T(8,128)} %get-tuple-element.21.g_ref, ...), custom_call_target="tpu_custom_call" | custom-call | tf_op jit(solution)/shard_map/pallas_call | solution.py:33
  35.4 35.8 %all_to_all.35.in_ref = bf16[64,8,128]{2,1,0:T(8,128)(2,1)} all-to-all(bf16[64,8,128]{2,1,0:T(8,128)(2,1)} %shard_map.115), channel_id=1, replica_groups=mesh['zh'=4,'z0'=2,'h'=2,'k'=2,'l'=4,'x'=4] {'z0','h','l','x'}, dimensions={0} | all-to-all | bytes 262144 | tf_op jit(solution)/shard_map/all_to_all | solution.py:196
  71.2 1.6 shard_map.116
  72.8 5.8 %all-to-all-start.1 = ((bf16[64,8,128]{2,1,0:T(8,128)(2,1)}), bf16[64,8,128]{2,1,0:T(8,128)(2,1)S(1)}, u32[]{:S(2)}, u32[]{:S(2)}) async-start(bf16[64,8,128]{2,1,0:T(8,128)(2,1)} %shard_map.116), calls=%async_computation.1 | async-start | bytes 262144 | tf_op jit(solution)/shard_map/all_to_all | solution.py:196
  78.6 0.6 slice.13.seen_other_ref
  79.2 11.0 %all-to-all-done.1.in_ref = bf16[64,8,128]{2,1,0:T(8,128)(2,1)S(1)} async-done(((bf16[64,8,128]{2,1,0:T(8,128)(2,1)}), bf16[64,8,128]{2,1,0:T(8,128)(2,1)S(1)}, u32[]{:S(2)}, u32[]{:S(2)}) %all-to-all-start.1) | async-done | bytes 131104 | tf_op jit(solution)/shard_map/all_to_all | solution.py:196
  90.2 0.7 copy-done.2
  90.8 2.9 %shard_map.117 = bf16[16,16,256]{2,1,0:T(8,128)(2,1)} custom-call(s32[5]{0:T(128)} %stack.37.at_ref, bf16[64,8,128]{2,1,0:T(8,128)(2,1)} %copy-done.2, bf16[768,1024]{1,0:T(8,128)(2,1)} %shard_map.114.own_ref, bf16[768,1024]{1,0:T(8,128)(2,1)} %copy-done, f32[16,128]{1,0:T(8,128)} %get-tuple-element.24.seen_ref, f32[16,128]{1,0:T(8,128)} %slice.13.seen_other_ref), custom_call_target="tpu_custom_call" | custom-call | tf_op jit(solution)/shard_map/pallas_call | solution.py:33
  93.7 3.5 %all-to-all-start.2 = ((bf16[16,16,256]{2,1,0:T(8,128)(2,1)}), bf16[16,16,256]{2,1,0:T(8,128)(2,1)S(1)}, u32[]{:S(2)}, u32[]{:S(2)}) async-start(bf16[16,16,256]{2,1,0:T(8,128)(2,1)} %shard_map.117), calls=%async_computation.2 | async-start | bytes 262144 | tf_op jit(solution)/shard_map/all_to_all | solution.py:196
  97.2 0.5 slice.14.noise_other_ref
  97.7 7.3 %all-to-all-done.2.in_ref = bf16[16,16,256]{2,1,0:T(8,128)(2,1)S(1)} async-done(((bf16[16,16,256]{2,1,0:T(8,128)(2,1)}), bf16[16,16,256]{2,1,0:T(8,128)(2,1)S(1)}, u32[]{:S(2)}, u32[]{:S(2)}) %all-to-all-start.2) | async-done | bytes 131104 | tf_op jit(solution)/shard_map/all_to_all | solution.py:196
  105.0 0.7 copy-done.1
  105.6 2.8 %shard_map.118 = (bf16[64,8,128]{2,1,0:T(8,128)(2,1)}, f32[16,128]{1,0:T(8,128)}, f32[16,128]{1,0:T(8,128)}, f32[16,1024]{1,0:T(8,128)}) custom-call(s32[5]{0:T(128)} %stack.37.at_ref, bf16[16,16,256]{2,1,0:T(8,128)(2,1)} %copy-done.1, bf16[768,1024]{1,0:T(8,128)(2,1)} %shard_map.114.own_ref, bf16[768,1024]{1,0:T(8,128)(2,1)} %copy-done, f32[1,128]{1,0:T(1,128)} %bitcast.12, ...), custom_call_target="tpu_custom_call" | custom-call | tf_op jit(solution)/shard_map/pallas_call | solution.py:33
  108.4 17.0 %all_to_all.36.in_ref = bf16[64,8,128]{2,1,0:T(8,128)(2,1)} all-to-all(bf16[64,8,128]{2,1,0:T(8,128)(2,1)} %get-tuple-element.14), channel_id=1, replica_groups=mesh['zh'=4,'z0'=2,'h'=2,'k'=2,'l'=4,'x'=4] {'zh','z0','h','l'}, dimensions={0} | all-to-all | bytes 262144 | tf_op jit(solution)/shard_map/all_to_all | solution.py:196
  125.4 1.6 shard_map.119
  127.0 15.3 %all_to_all.37.in_ref = bf16[64,8,128]{2,1,0:T(8,128)(2,1)} all-to-all(bf16[64,8,128]{2,1,0:T(8,128)(2,1)} %shard_map.119), channel_id=1, replica_groups=mesh['zh'=4,'z0'=2,'h'=2,'k'=2,'l'=4,'x'=4] {'z0','h','l','x'}, dimensions={0} | all-to-all | bytes 262144 | tf_op jit(solution)/shard_map/all_to_all | solution.py:196
  142.3 3.0 %shard_map.120 = bf16[64,8,128]{2,1,0:T(8,128)(2,1)} custom-call(s32[5]{0:T(128)} %stack.37.at_ref, bf16[64,8,128]{2,1,0:T(8,128)(2,1)} %all_to_all.37.in_ref, bf16[768,1024]{1,0:T(8,128)(2,1)} %shard_map.114.own_ref, bf16[768,1024]{1,0:T(8,128)(2,1)} %copy-done, f32[16,1024]{1,0:T(8,128)} %get-tuple-element.15.force_ref), custom_call_target="tpu_custom_call" | custom-call | tf_op jit(solution)/shard_map/pallas_call | solution.py:33
  145.3 16.9 %all_to_all.38.in_ref = bf16[64,8,128]{2,1,0:T(8,128)(2,1)} all-to-all(bf16[64,8,128]{2,1,0:T(8,128)(2,1)} %shard_map.120), channel_id=1, replica_groups=mesh['zh'=4,'z0'=2,'h'=2,'k'=2,'l'=4,'x'=4] {'zh','z0','h','l'}, dimensions={0} | all-to-all | bytes 262144 | tf_op jit(solution)/shard_map/all_to_all | solution.py:196
  162.2 1.6 shard_map.121
  163.8 4.6 %all-to-all-start.6 = ((bf16[64,8,128]{2,1,0:T(8,128)(2,1)}), bf16[64,8,128]{2,1,0:T(8,128)(2,1)S(1)}, u32[]{:S(2)}, u32[]{:S(2)}) async-start(bf16[64,8,128]{2,1,0:T(8,128)(2,1)} %shard_map.121), calls=%async_computation.6 | async-start | bytes 262144 | tf_op jit(solution)/shard_map/all_to_all | solution.py:196
  168.4 9.0 %collective-permute-start.5 = (f32[16,128]{1,0:T(8,128)S(1)}, f32[16,128]{1,0:T(8,128)S(1)}, u32[]{:S(2)}, u32[]{:S(2)}) collective-permute-start(f32[16,128]{1,0:T(8,128)S(1)} %copy-done.10), channel_id=1, source_target_pairs={{0,16},{16,0},{1,17},{17,1},{2,18},{18,2},{3,19},{19,3},{4,20},{20... | collective-permute-start | bytes 24584 | tf_op jit(solution)/shard_map/ppermute | solution.py:192
  177.4 1.0 all-to-all-done.6.in_ref
  178.4 0.7 copy-done.3
  179.0 1.6 shard_map.122
  180.6 10.1 %collective-permute-start.4 = (f32[16,512]{1,0:T(8,128)}, f32[16,512]{1,0:T(8,128)S(1)}, u32[]{:S(2)}, u32[]{:S(2)}) collective-permute-start(f32[16,512]{1,0:T(8,128)} %get-tuple-element.17), channel_id=1, source_target_pairs={{0,16},{16,0},{1,17},{17,1},{2,18},{18,2},{3,19},{19,3},{4,20},{20... | collective-permute-start | bytes 98312 | tf_op jit(solution)/shard_map/ppermute | solution.py:192
  190.7 0.6 maximum_select_fusion
  191.4 0.4 collective-permute-done.4.theirs_ref
  191.8 0.6 copy-done.4
  192.4 2.2 %shard_map.123 = f32[32,4,128]{2,1,0:T(4,128)} custom-call(s32[5]{0:T(128)} %stack.37.at_ref, f32[16,512]{1,0:T(8,128)} %get-tuple-element.16.mine_ref, f32[16,512]{1,0:T(8,128)} %copy-done.4, f32[4,128,128]{2,1,0:T(8,128)} %inverse_ref.5, f32[4,128]{1,0:T(4,128)} %log_ref.3, f32[4,128]{1,0:T(4,128)} %base_ref.3), custom_call_target="tpu_custom_call" | custom-call | tf_op jit(solution)/shard_map/pallas_call | solution.py:33
  (20 shorter events, 0.0 us)
Async XLA Ops:
  3.3 14.5 %copy-start.9 = (f32[128]{0:T(128)S(1)}, f32[128]{0:T(128)}, u32[]{:S(2)}) copy-start(f32[128]{0:T(128)} %param.19) | copy-start | bytes 1540
  3.3 14.5 %copy-start.8 = (s32[128]{0:T(128)S(1)}, s32[128]{0:T(128)}, u32[]{:S(2)}) copy-start(s32[128]{0:T(128)} %param.17) | copy-start | bytes 1540
  9.1 21.9 %collective-permute-start.2 = (bf16[768,1024]{1,0:T(8,128)(2,1)}, bf16[768,1024]{1,0:T(8,128)(2,1)S(1)}, u32[]{:S(2)}, u32[]{:S(2)}) collective-permute-start(bf16[768,1024]{1,0:T(8,128)(2,1)} %shard_map.114.own_ref), channel_id=1, source_target_pairs={{0,16},{16,0},{1,17},{17,1},{2,18},{18,2},{3,19},{19,3},{4,20},{20... | collective-permute-start | bytes 4718600 | tf_op jit(solution)/shard_map/ppermute | solution.py:192
  24.0 6.4 %collective-permute-start.3 = (f32[16,768]{1,0:T(8,128)S(1)}, f32[16,768]{1,0:T(8,128)S(1)}, u32[]{:S(2)}, u32[]{:S(2)}) collective-permute-start(f32[16,768]{1,0:T(8,128)S(1)} %maximum_maximum_fusion), channel_id=1, source_target_pairs={{0,16},{16,0},{1,17},{17,1},{2,18},{18,2},{3,19},{19,3},{4,20},{20... | collective-permute-start | bytes 147464 | tf_op jit(solution)/shard_map/ppermute | solution.py:192
  26.6 4.4 %collective-permute-start = (bf16[16,512]{1,0:T(8,128)(2,1)S(1)}, bf16[16,512]{1,0:T(8,128)(2,1)S(1)}, u32[]{:S(2)}, u32[]{:S(2)}) collective-permute-start(bf16[16,512]{1,0:T(8,128)(2,1)S(1)} %get-tuple-element.23), channel_id=1, source_target_pairs={{0,0},{1,32},{2,64},{3,96},{4,128},{5,160},{6,192},{7,224},{8,256}... | collective-permute-start | bytes 49160 | tf_op jit(solution)/shard_map/ppermute | solution.py:217
  27.3 3.7 %collective-permute-start.1 = (bf16[16,512]{1,0:T(8,128)(2,1)S(1)}, bf16[16,512]{1,0:T(8,128)(2,1)S(1)}, u32[]{:S(2)}, u32[]{:S(2)}) collective-permute-start(bf16[16,512]{1,0:T(8,128)(2,1)S(1)} %get-tuple-element.22), channel_id=1, source_target_pairs={{0,16},{1,48},{2,80},{3,112},{4,144},{5,176},{6,208},{7,240},{8,27... | collective-permute-start | bytes 49160 | tf_op jit(solution)/shard_map/ppermute | solution.py:218
  31.0 0.6 copy-start.5
  31.0 0.6 copy-start.6
  31.0 1.1 copy-start
  72.8 17.4 %all-to-all-start.1 = ((bf16[64,8,128]{2,1,0:T(8,128)(2,1)}), bf16[64,8,128]{2,1,0:T(8,128)(2,1)S(1)}, u32[]{:S(2)}, u32[]{:S(2)}) async-start(bf16[64,8,128]{2,1,0:T(8,128)(2,1)} %shard_map.116), calls=%async_computation.1 | async-start | bytes 262144 | tf_op jit(solution)/shard_map/all_to_all | solution.py:196
  90.2 0.7 copy-start.2
  93.7 11.3 %all-to-all-start.2 = ((bf16[16,16,256]{2,1,0:T(8,128)(2,1)}), bf16[16,16,256]{2,1,0:T(8,128)(2,1)S(1)}, u32[]{:S(2)}, u32[]{:S(2)}) async-start(bf16[16,16,256]{2,1,0:T(8,128)(2,1)} %shard_map.117), calls=%async_computation.2 | async-start | bytes 262144 | tf_op jit(solution)/shard_map/all_to_all | solution.py:196
  105.0 0.7 copy-start.1
  142.3 26.2 %copy-start.10 = (f32[16,128]{1,0:T(8,128)S(1)}, f32[16,128]{1,0:T(8,128)}, u32[]{:S(2)}) copy-start(f32[16,128]{1,0:T(8,128)} %get-tuple-element.19) | copy-start | bytes 24580
  142.3 48.5 %copy-start.7 = (f32[16,128]{1,0:T(8,128)S(1)}, f32[16,128]{1,0:T(8,128)}, u32[]{:S(2)}) copy-start(f32[16,128]{1,0:T(8,128)} %get-tuple-element.18) | copy-start | bytes 24580
  163.8 14.6 %all-to-all-start.6 = ((bf16[64,8,128]{2,1,0:T(8,128)(2,1)}), bf16[64,8,128]{2,1,0:T(8,128)(2,1)S(1)}, u32[]{:S(2)}, u32[]{:S(2)}) async-start(bf16[64,8,128]{2,1,0:T(8,128)(2,1)} %shard_map.121), calls=%async_computation.6 | async-start | bytes 262144 | tf_op jit(solution)/shard_map/all_to_all | solution.py:196
  168.4 22.3 %collective-permute-start.5 = (f32[16,128]{1,0:T(8,128)S(1)}, f32[16,128]{1,0:T(8,128)S(1)}, u32[]{:S(2)}, u32[]{:S(2)}) collective-permute-start(f32[16,128]{1,0:T(8,128)S(1)} %copy-done.10), channel_id=1, source_target_pairs={{0,16},{16,0},{1,17},{17,1},{2,18},{18,2},{3,19},{19,3},{4,20},{20... | collective-permute-start | bytes 24584 | tf_op jit(solution)/shard_map/ppermute | solution.py:192
  178.4 0.7 copy-start.3
  180.6 11.2 %collective-permute-start.4 = (f32[16,512]{1,0:T(8,128)}, f32[16,512]{1,0:T(8,128)S(1)}, u32[]{:S(2)}, u32[]{:S(2)}) collective-permute-start(f32[16,512]{1,0:T(8,128)} %get-tuple-element.17), channel_id=1, source_target_pairs={{0,16},{16,0},{1,17},{17,1},{2,18},{18,2},{3,19},{19,3},{4,20},{20... | collective-permute-start | bytes 98312 | tf_op jit(solution)/shard_map/ppermute | solution.py:192
  191.8 0.6 copy-start.4

commit v2 on v1

v2 whole, which is shorter than its diff:
```python
import jax
import jax.numpy as jnp
from jax import lax
from jax.experimental import pallas as pl
from jax.experimental.pallas import tpu as pltpu
from jax.sharding import Mesh
from jax.sharding import PartitionSpec as P

AXES = ("zh", "z0", "h", "k", "l", "x")
SIZES = (4, 2, 2, 2, 4, 4)
ROW = ("zh", "z0", "h", "k")
COL = ("l", "x")
NEAR = ("z0", "h", "l", "x")
FAR = ("zh", "z0", "h", "l")
F32 = jnp.float32
BF16 = jnp.bfloat16
HIGHEST = lax.Precision.HIGHEST
VMEM = pl.BlockSpec(memory_space=pltpu.VMEM)
SMEM = pl.BlockSpec(memory_space=pltpu.SMEM)

GRANT = 12 * 2**20


def split(array):
    high = array.astype(BF16)
    return high, (array - high.astype(F32)).astype(BF16)


def matmul(a, b, precision=None):
    return lax.dot_general(a, b, (((1,), (0,)), ((), ())), precision=precision, preferred_element_type=F32)


def matmul_t(a, b, precision=None):
    return lax.dot_general(a, b, (((1,), (1,)), ((), ())), precision=precision, preferred_element_type=F32)


def call(kernel, outs, arrays, scratch=(), scalars=(), cost=None):
    return pl.pallas_call(
        kernel,
        out_shape=[jax.ShapeDtypeStruct(shape, dtype) for shape, dtype in outs],
        in_specs=[SMEM] * len(scalars) + [VMEM] * len(arrays),
        out_specs=[VMEM] * len(outs),
        scratch_shapes=list(scratch),
        cost_estimate=cost,
        compiler_params=pltpu.CompilerParams(vmem_limit_bytes=GRANT),
    )(*scalars, *arrays)


def cross_index():
    return lax.axis_index("z0") * 2 + lax.axis_index("h")


def of_core(core, rows=16):
    return pl.ds(pl.multiple_of(core * rows, rows), rows)


def first_state(inverse_ref, log_ref, base_ref, direction_ref, g_ref, first_ref, second_ref):
    core = lax.axis_index("k")
    alpha_u = jnp.exp(log_ref[...]) * base_ref[...]
    for q in range(4):
        forcing = -alpha_u[q][None, :] * direction_ref[:, q, :]
        g_ref[:, q * 128 : (q + 1) * 128] = matmul_t(forcing, inverse_ref[q], HIGHEST)
    first_ref[...] = g_ref[of_core(core), :].astype(BF16)
    second_ref[...] = g_ref[of_core(1 - core), :].astype(BF16)


def build(columns_ref, counts_ref, blocks_ref, inverse_ref, weight_ref, rows_ref, noise_ref, g_ref, out_ref, seen_ref, dense):
    core = lax.axis_index("k")
    for q in range(4):
        dense[...] = jnp.zeros(dense.shape, F32)

        def add(slot, carry):
            lanes = pl.ds(pl.multiple_of(columns_ref[q, slot] * 128, 128), 128)
            dense[:, lanes] += blocks_ref[q, slot].astype(F32)
            return carry

        lax.fori_loop(0, counts_ref[q], add, 0)
        high, low = split(dense[...])
        inverse, inverse_low = split(inverse_ref[q])
        out_ref[q * 128 : (q + 1) * 128, :] = (
            matmul(inverse, high) + matmul(inverse, low) + matmul(inverse_low, high)
        ).astype(BF16)
    rows = rows_ref[...]
    rows_down = jnp.transpose(jnp.broadcast_to(rows.astype(F32), (128, 128)))
    weight = weight_ref[...]
    for q in range(4):
        out_ref[640:768, q * 128 : (q + 1) * 128] = jnp.where(rows_down == q, weight, 0.0).astype(BF16)
    out_ref[512:640, :] = matmul(out_ref[640:768, 0:512], out_ref[0:512, :]).astype(BF16)
    seen = jnp.zeros(seen_ref.shape, F32)
    for q in range(4):
        seen += jnp.where(rows == q, matmul_t(g_ref[:, q * 128 : (q + 1) * 128], weight, HIGHEST), 0.0)
    seen_ref[...] = seen
    out_ref[640:656, 512:1024], out_ref[656:672, 512:1024] = split(g_ref[of_core(1 - core), :])
    out_ref[672:688, 512:640], out_ref[672:688, 640:768] = split(seen_ref[of_core(1 - core), :])
    out_ref[672:688, 768:896], out_ref[672:688, 896:1024] = split(jnp.broadcast_to(noise_ref[...], (16, 128)))
    out_ref[688:768, 512:1024] = jnp.zeros((80, 512), BF16)


def joined(ref, rows, lanes, rows_low, lanes_low):
    return ref[rows, lanes].astype(F32) + ref[rows_low, lanes_low].astype(F32)


def put_tiles(out_ref, values, first_block, near):
    for q in range(values.shape[1] // 128):
        for half in range(2):
            tile = values[half * 8 : half * 8 + 8, q * 128 : (q + 1) * 128].astype(BF16)
            share = (first_block + q) * 2 + half
            for copy in range(4):
                out_ref[share * 4 + copy if near else copy * 16 + share] = tile


def forward_one(first_ref, second_ref, own_ref, other_ref, g_ref, out_ref, state):
    core = lax.axis_index("k")
    state[:, of_core(core, 512)] = first_ref[...]
    state[:, of_core(1 - core, 512)] = second_ref[...]
    low = state[...]
    g_mine = g_ref[of_core(core), :]
    g_other = joined(other_ref, slice(640, 656), slice(512, 1024), slice(656, 672), slice(512, 1024))
    put_tiles(out_ref, g_mine * (1.0 / 16) - matmul_t(low, own_ref[0:512, :]), core * 4, True)
    put_tiles(out_ref, g_other * (1.0 / 16) - matmul_t(low, other_ref[0:512, :]), (1 - core) * 4, True)


def sum_near(in_ref, out_ref):
    first = lax.axis_index("x") * 16
    total = in_ref[first].astype(F32)
    for source in range(1, 16):
        total += in_ref[first + source].astype(F32)
    out_ref[...] = jnp.broadcast_to(total.astype(BF16)[None], out_ref.shape)


def sum_far(in_ref, out_ref):
    first = lax.axis_index("zh")
    total = in_ref[first].astype(F32)
    for source in range(1, 16):
        total += in_ref[first + 4 * source].astype(F32)
    out_ref[...] = jnp.broadcast_to(total.astype(BF16)[None], out_ref.shape)


def forward_two(in_ref, own_ref, other_ref, seen_ref, out_ref, state):
    core = lax.axis_index("k")
    first = lax.axis_index("l") * 16
    for block in range(8):
        for half in range(2):
            state[half * 8 : half * 8 + 8, block * 128 : (block + 1) * 128] = in_ref[first + block * 2 + half].astype(F32)
    low = state[...].astype(BF16)
    seen_other = joined(other_ref, slice(672, 688), slice(512, 640), slice(672, 688), slice(640, 768))
    mine = seen_ref[of_core(core), :] * (1.0 / 16) - matmul_t(low, own_ref[512:640, :])
    theirs = seen_other * (1.0 / 16) - matmul_t(low, other_ref[512:640, :])
    out_ref[:, :, 0:128] = jnp.broadcast_to(mine.astype(BF16)[None], (16, 16, 128))
    out_ref[:, :, 128:256] = jnp.broadcast_to(theirs.astype(BF16)[None], (16, 16, 128))


def adjoint_one(in_ref, own_ref, other_ref, noise_ref, out_ref, predicted_ref, force_ref):
    predicted = in_ref[0].astype(F32)
    for source in range(1, 16):
        predicted += in_ref[source].astype(F32)
    predicted_ref[...] = predicted
    noise_other = joined(other_ref, slice(672, 688), slice(768, 896), slice(672, 688), slice(896, 1024))
    scaled = (predicted[:, 0:128] * noise_ref[...]).astype(BF16)
    scaled_other = (predicted[:, 128:256] * noise_other).astype(BF16)
    put_tiles(out_ref, matmul(scaled, own_ref[512:640, :]) + matmul(scaled_other, other_ref[512:640, :]), 0, False)
    force_ref[:, 0:512] = -matmul(scaled, own_ref[640:768, 0:512])
    force_ref[:, 512:1024] = -matmul(scaled_other, other_ref[640:768, 0:512])


def gather_rows(in_ref, force_ref, state):
    core, cross = lax.axis_index("k"), cross_index()
    for side in range(2):
        first_block = (core if side == 0 else 1 - core) * 4
        for q in range(4):
            lanes = slice(side * 512 + q * 128, side * 512 + (q + 1) * 128)
            for half in range(2):
                share = (first_block + q) * 2 + half
                state[half * 8 : half * 8 + 8, lanes] = (
                    force_ref[half * 8 : half * 8 + 8, lanes] + in_ref[share * 4 + cross].astype(F32)
                )


def adjoint_two(in_ref, own_ref, other_ref, force_ref, out_ref, state):
    gather_rows(in_ref, force_ref, state)
    low = state[...].astype(BF16)
    total = matmul(low[:, 0:512], own_ref[0:512, :]) + matmul(low[:, 512:1024], other_ref[0:512, :])
    put_tiles(out_ref, -total, 0, False)


def adjoint_end(in_ref, force_ref, predicted_ref, mine_ref, theirs_ref, state):
    gather_rows(in_ref, force_ref, state)
    mine_ref[...] = state[:, 0:512]
    theirs_ref[:, 0:512] = state[:, 512:1024]
    theirs_ref[:, 512:640] = predicted_ref[:, 128:256]


def finish(mine_ref, came_ref, predicted_ref, inverse_ref, log_ref, base_ref, out_ref, seen_ref):
    alpha_u = jnp.exp(log_ref[...]) * base_ref[...]
    core = lax.axis_index("k")
    seen_ref[of_core(core), :] = predicted_ref[:, 0:128]
    seen_ref[of_core(1 - core), :] = came_ref[:, 512:640]
    for part, ref in ((core, mine_ref), (1 - core, came_ref)):
        for q in range(4):
            adjoint = matmul(ref[:, q * 128 : (q + 1) * 128], inverse_ref[q], HIGHEST)
            out_ref[of_core(part), q, :] = -alpha_u[q][None, :] * adjoint


def transposed(flip):
    pairs = []
    for zh in range(4):
        for cross in range(4):
            for k in range(2):
                for l in range(4):
                    for x in range(4):
                        source = (((zh * 4 + cross) * 2 + k) * 4 + l) * 4 + x
                        target = (((l * 4 + x) * 2 + (k ^ flip)) * 4 + zh) * 4 + cross
                        pairs.append((source, target))
    return pairs


def swapped(array):
    return lax.ppermute(array, "k", [(0, 1), (1, 0)])


def exchange(array, axes):
    return lax.all_to_all(array, axes, split_axis=0, concat_axis=0, tiled=True)


def per_device(
    blocks, columns, counts, inverse_diag, log_inverse_permeability, base_velocity, direction, obs_rows, obs_weight, noise_prec
):
    rows, noise = obs_rows.reshape(1, 128), noise_prec.reshape(1, 128)
    tiles = ((64, 8, 128), BF16)
    low_state = [pltpu.VMEM((16, 1024), BF16)]
    full_state = [pltpu.VMEM((16, 1024), F32)]

    g, first, second = call(
        first_state,
        [((32, 512), F32), ((16, 512), BF16), ((16, 512), BF16)],
        [inverse_diag, log_inverse_permeability, base_velocity, direction],
    )
    first = lax.ppermute(first, AXES, transposed(0))
    second = lax.ppermute(second, AXES, transposed(1))
    own, seen = call(
        build,
        [((768, 1024), BF16), ((32, 128), F32)],
        [blocks, inverse_diag, obs_weight, rows, noise, g],
        [pltpu.VMEM((128, 1024), F32)],
        [columns, counts.reshape(4)],
        pl.CostEstimate(flops=2 * 10**9, bytes_accessed=4 * 10**6, transcendentals=0),
    )
    other = swapped(own)

    (part,) = call(forward_one, [tiles], [first, second, own, other, g], low_state)
    (part,) = call(sum_near, [tiles], [exchange(part, NEAR)])
    (part,) = call(forward_two, [((16, 16, 256), BF16)], [exchange(part, FAR), own, other, seen], full_state)
    part, predicted, force = call(
        adjoint_one,
        [tiles, ((16, 256), F32), ((16, 1024), F32)],
        [exchange(part, COL), own, other, noise],
    )
    (part,) = call(sum_far, [tiles], [exchange(part, FAR)])
    (part,) = call(adjoint_two, [tiles], [exchange(part, NEAR), own, other, force], full_state)
    (part,) = call(sum_far, [tiles], [exchange(part, FAR)])
    mine, theirs = call(
        adjoint_end, [((16, 512), F32), ((16, 640), F32)], [exchange(part, NEAR), force, predicted], full_state
    )
    return tuple(
        call(
            finish,
            [((32, 4, 128), F32), ((32, 128), F32)],
            [mine, swapped(theirs), predicted, inverse_diag, log_inverse_permeability, base_velocity],
        )
    )


def solution(mesh):
    grid = Mesh(mesh.devices.reshape(SIZES), AXES)
    return jax.shard_map(
        per_device,
        mesh=grid,
        in_specs=(
            P(ROW, COL, None, None),
            P(ROW, COL),
            P(ROW, COL),
            P(ROW, None, None),
            P(ROW, None),
            P(ROW, None),
            P(None, ROW, None),
            P(ROW),
            P(ROW, None),
            P(ROW),
        ),
        out_specs=(P(None, ROW, None), P(None, ROW)),
        check_vma=False,
    )
```

time: 196 us -> 164 us (0.84)
  blocking collectives: 84.9 us -> 123 us
  starting transfers between devices: 46.7 us -> 22 us
  Pallas kernels: 29.1 us -> 6.75 us
  waiting for transfers between devices: 19.6 us -> 1.99 us
  local copies, waits for them, and re-layouts: 10.8 us -> 8.08 us
  other arithmetic: 2.58 us -> 0 us
    all_to_all x4 -> x7, blocking collectives: 84.9 us -> 123 us  [exchange(): return lax.all_to_all(array, axes, split_axis=0, concat_axis=0, tiled=True)]
    pallas_call x11, Pallas kernels: 29.1 us -> 6.75 us  [call(): pl.pallas_call(kernel, out_shape=[jax.ShapeDtypeStruct(shape, dtype) for...]
    all_to_all x3 -> x0, waiting for transfers between devices: 19.2 us -> none  [exchange(): return lax.all_to_all(array, axes, split_axis=0, concat_axis=0, tiled=True)]
    all_to_all x3 -> x0, starting transfers between devices: 13.9 us -> none  [exchange(): return lax.all_to_all(array, axes, split_axis=0, concat_axis=0, tiled=True)]
    ppermute x4 -> x2, starting transfers between devices: 29.7 us -> 19.4 us  [swapped(): return lax.ppermute(array, 'k', [(0, 1), (1, 0)])]
    dynamic_slice x3 -> x0, local copies, waits for them, and re-layouts: 3.44 us -> none  [half(): return lax.dynamic_slice_in_dim(array, which * 16, 16, 0)]
    unnamed x23 -> x26, local copies, waits for them, and re-layouts: 5.05 us -> 8.08 us
    convert_element_type x2 -> x0, other arithmetic: 1.96 us -> none  [the longest x1 1.37 us: per_device(): onehot_t = (obs_rows[:, None] == jnp.arange(4)[None, :]).astype(F32)]
  transfers between devices with their start and end apart: 9 -> 4, of which waited for: 4 -> 2; matrix products, arithmetic and copies ran while one was open for 4% -> 0% of each run, Pallas kernels for 2% -> 0%
where the time goes in v2:
time: 164 us; the launch traced here: 163 us
  blocking collectives  123 us (75%)
  starting transfers between devices  22 us (13%)
  local copies, waits for them, and re-layouts  8.08 us (5%)
  Pallas kernels  6.75 us (4%)
  waiting for transfers between devices  1.99 us (1%)
    all_to_all x7, blocking collectives, exchange(): return lax.all_to_all(array, axes, split_axis=0, concat_axis=0, tiled=True)  123 us
    ppermute x2, starting transfers between devices, swapped(): return lax.ppermute(array, 'k', [(0, 1), (1, 0)])  19.4 us
    unnamed x26, local copies, waits for them, and re-layouts  8.08 us
    pallas_call x11, Pallas kernels, call(): pl.pallas_call(kernel, out_shape=[jax.ShapeDtypeStruct(shape, dtype) for...  6.75 us
  transfers between devices with their start and end apart: 4, of which 2 were waited for; matrix products, arithmetic and copies ran while one was open for 0% of the time, Pallas kernels for 0%

profile of v2, /device:TPU:1, one launch (start us, length us, event | category | flops | bytes accessed | tf_op | source)
XLA Modules:
  0.0 162.9 jit_solution(13352484290647573890)
XLA Ops:
  0.6 0.0 copy-start
  0.6 0.9 copy-done
  1.6 0.0 copy-start.2
  1.6 0.8 copy-done.2
  2.4 0.0 copy-start.3
  2.4 0.7 copy-done.3
  3.1 0.0 copy-start.5
  3.1 0.7 copy-done.5
  3.8 0.5 shard_map.113
  4.3 0.0 copy-start.7
  4.3 0.7 copy-done.7
  5.0 0.0 copy-start.8
  5.0 1.4 copy-done.8
  6.4 0.0 copy-start.9
  6.4 0.8 copy-done.9
  7.2 0.0 copy-start.10
  7.2 0.7 copy-done.10
  7.9 0.0 copy-start.11
  7.9 0.7 copy-done.11
  8.6 0.0 copy-start.12
  8.6 0.7 copy-done.12
  9.2 3.4 %shard_map.114 = (bf16[768,1024]{1,0:T(8,128)(2,1)S(1)}, f32[32,128]{1,0:T(8,128)S(1)}) custom-call(s32[4,12]{1,0:T(4,128)S(1)} %copy-done.10, s32[4]{0:T(128)S(1)} %bitcast.5, bf16[4,12,128,128]{3,2,1,0:T(8,128)(2,1)S(1)} %copy-done.8, f32[4,128,128]{2,1,0:T(8,128)S(1)} %copy-done, f32[128,128]{1,0:T(8,128)S(1)} %copy-done.9, s32[1,128]{1,0:T(1,128)S(1)} %bitcast.6, ...), custom_call_target="tpu_custom_call" | custom-call | flops 2000000000 | bytes 4000000 | tf_op jit(solution)/shard_map/pallas_call | solution.py:38
  12.6 8.8 %collective-permute-start.2 = (bf16[768,1024]{1,0:T(8,128)(2,1)S(1)}, bf16[768,1024]{1,0:T(8,128)(2,1)S(1)}, u32[]{:S(2)}, u32[]{:S(2)}) collective-permute-start(bf16[768,1024]{1,0:T(8,128)(2,1)S(1)} %get-tuple-element.15.own_ref), channel_id=1, source_target_pairs={{0,16},{16,0},{1,17},{17,1},{2,18},{18,2},{3,19},{19,3},{4,20},{20... | collective-permute-start | bytes 4718600 | tf_op jit(solution)/shard_map/ppermute | solution.py:218
  21.4 0.7 collective-permute-start
  22.1 1.9 %collective-permute-start.1 = (bf16[16,512]{1,0:T(8,128)(2,1)S(1)}, bf16[16,512]{1,0:T(8,128)(2,1)S(1)}, u32[]{:S(2)}, u32[]{:S(2)}) collective-permute-start(bf16[16,512]{1,0:T(8,128)(2,1)S(1)} %get-tuple-element.13), channel_id=1, source_target_pairs={{0,16},{1,48},{2,80},{3,112},{4,144},{5,176},{6,208},{7,240},{8,27... | collective-permute-start | bytes 49160 | tf_op jit(solution)/shard_map/ppermute | solution.py:239
  24.0 0.0 collective-permute-done.first_ref
  24.0 1.1 collective-permute-done.1.second_ref
  25.2 0.0 collective-permute-done.2.other_ref
  25.2 0.7 shard_map.115
  25.8 35.7 %all_to_all.35.in_ref = bf16[64,8,128]{2,1,0:T(8,128)(2,1)S(1)} all-to-all(bf16[64,8,128]{2,1,0:T(8,128)(2,1)S(1)} %shard_map.115), channel_id=1, replica_groups=mesh['zh'=4,'z0'=2,'h'=2,'k'=2,'l'=4,'x'=4] {'z0','h','l','x'}, dimensions={0} | all-to-all | bytes 262144 | tf_op jit(solution)/shard_map/all_to_all | solution.py:222
  61.5 17.6 %all_to_all.36.in_ref = bf16[64,8,128]{2,1,0:T(8,128)(2,1)S(1)} all-to-all(bf16[64,8,128]{2,1,0:T(8,128)(2,1)S(1)} %shard_map.116), channel_id=1, replica_groups=mesh['zh'=4,'z0'=2,'h'=2,'k'=2,'l'=4,'x'=4] {'zh','z0','h','l'}, dimensions={0} | all-to-all | bytes 262144 | tf_op jit(solution)/shard_map/all_to_all | solution.py:222
  79.1 0.3 shard_map.117
  79.4 10.4 %all_to_all.37.in_ref = bf16[16,16,256]{2,1,0:T(8,128)(2,1)S(1)} all-to-all(bf16[16,16,256]{2,1,0:T(8,128)(2,1)S(1)} %shard_map.117), channel_id=1, replica_groups=mesh['zh'=4,'z0'=2,'h'=2,'k'=2,'l'=4,'x'=4] {'l','x'}, dimensions={0} | all-to-all | bytes 262144 | tf_op jit(solution)/shard_map/all_to_all | solution.py:222
  89.8 0.2 shard_map.118
  90.0 16.6 %all_to_all.38.in_ref = bf16[64,8,128]{2,1,0:T(8,128)(2,1)S(1)} all-to-all(bf16[64,8,128]{2,1,0:T(8,128)(2,1)S(1)} %get-tuple-element.17), channel_id=1, replica_groups=mesh['zh'=4,'z0'=2,'h'=2,'k'=2,'l'=4,'x'=4] {'zh','z0','h','l'}, dimensions={0} | all-to-all | bytes 262144 | tf_op jit(solution)/shard_map/all_to_all | solution.py:222
  106.7 13.8 %all_to_all.39.in_ref = bf16[64,8,128]{2,1,0:T(8,128)(2,1)S(1)} all-to-all(bf16[64,8,128]{2,1,0:T(8,128)(2,1)S(1)} %shard_map.119), channel_id=1, replica_groups=mesh['zh'=4,'z0'=2,'h'=2,'k'=2,'l'=4,'x'=4] {'z0','h','l','x'}, dimensions={0} | all-to-all | bytes 262144 | tf_op jit(solution)/shard_map/all_to_all | solution.py:222
  120.5 0.0 copy-start.1
  120.5 0.0 copy-start.4
  120.5 0.0 copy-start.6
  120.5 0.4 shard_map.120
  120.9 15.3 %all_to_all.40.in_ref = bf16[64,8,128]{2,1,0:T(8,128)(2,1)S(1)} all-to-all(bf16[64,8,128]{2,1,0:T(8,128)(2,1)S(1)} %shard_map.120), channel_id=1, replica_groups=mesh['zh'=4,'z0'=2,'h'=2,'k'=2,'l'=4,'x'=4] {'zh','z0','h','l'}, dimensions={0} | all-to-all | bytes 262144 | tf_op jit(solution)/shard_map/all_to_all | solution.py:222
  136.2 14.0 %all_to_all.41.in_ref = bf16[64,8,128]{2,1,0:T(8,128)(2,1)S(1)} all-to-all(bf16[64,8,128]{2,1,0:T(8,128)(2,1)S(1)} %shard_map.121), channel_id=1, replica_groups=mesh['zh'=4,'z0'=2,'h'=2,'k'=2,'l'=4,'x'=4] {'z0','h','l','x'}, dimensions={0} | all-to-all | bytes 262144 | tf_op jit(solution)/shard_map/all_to_all | solution.py:222
  150.2 10.6 %collective-permute-start.3 = (f32[16,640]{1,0:T(8,128)S(1)}, f32[16,640]{1,0:T(8,128)S(1)}, u32[]{:S(2)}, u32[]{:S(2)}) collective-permute-start(f32[16,640]{1,0:T(8,128)S(1)} %get-tuple-element.21), channel_id=1, source_target_pairs={{0,16},{16,0},{1,17},{17,1},{2,18},{18,2},{3,19},{19,3},{4,20},{20... | collective-permute-start | bytes 122888 | tf_op jit(solution)/shard_map/ppermute | solution.py:218
  160.8 0.8 collective-permute-done.3.came_ref
  161.7 0.0 copy-done.1
  161.7 0.0 copy-done.4
  161.7 0.0 copy-done.6
  161.7 1.2 shard_map.123
  (4 shorter events, 0.1 us)
Async XLA Ops:
  0.6 1.0 copy-start
  1.6 0.8 copy-start.2
  2.4 0.7 copy-start.3
  3.1 0.7 copy-start.5
  4.3 0.7 copy-start.7
  5.0 1.4 copy-start.8
  6.4 0.8 copy-start.9
  7.2 0.7 copy-start.10
  7.9 0.7 copy-start.11
  8.6 0.7 copy-start.12
  12.6 12.5 %collective-permute-start.2 = (bf16[768,1024]{1,0:T(8,128)(2,1)S(1)}, bf16[768,1024]{1,0:T(8,128)(2,1)S(1)}, u32[]{:S(2)}, u32[]{:S(2)}) collective-permute-start(bf16[768,1024]{1,0:T(8,128)(2,1)S(1)} %get-tuple-element.15.own_ref), channel_id=1, source_target_pairs={{0,16},{16,0},{1,17},{17,1},{2,18},{18,2},{3,19},{19,3},{4,20},{20... | collective-permute-start | bytes 4718600 | tf_op jit(solution)/shard_map/ppermute | solution.py:218
  21.4 2.6 %collective-permute-start = (bf16[16,512]{1,0:T(8,128)(2,1)S(1)}, bf16[16,512]{1,0:T(8,128)(2,1)S(1)}, u32[]{:S(2)}, u32[]{:S(2)}) collective-permute-start(bf16[16,512]{1,0:T(8,128)(2,1)S(1)} %get-tuple-element.12), channel_id=1, source_target_pairs={{0,0},{1,32},{2,64},{3,96},{4,128},{5,160},{6,192},{7,224},{8,256}... | collective-permute-start | bytes 49160 | tf_op jit(solution)/shard_map/ppermute | solution.py:238
  22.1 3.1 %collective-permute-start.1 = (bf16[16,512]{1,0:T(8,128)(2,1)S(1)}, bf16[16,512]{1,0:T(8,128)(2,1)S(1)}, u32[]{:S(2)}, u32[]{:S(2)}) collective-permute-start(bf16[16,512]{1,0:T(8,128)(2,1)S(1)} %get-tuple-element.13), channel_id=1, source_target_pairs={{0,16},{1,48},{2,80},{3,112},{4,144},{5,176},{6,208},{7,240},{8,27... | collective-permute-start | bytes 49160 | tf_op jit(solution)/shard_map/ppermute | solution.py:239
  120.5 41.2 %copy-start.1 = (f32[4,128,128]{2,1,0:T(8,128)S(1)}, f32[4,128,128]{2,1,0:T(8,128)}, u32[]{:S(2)}) copy-start(f32[4,128,128]{2,1,0:T(8,128)} %inverse_ref.5) | copy-start | bytes 786436
  120.5 41.2 %copy-start.4 = (f32[4,128]{1,0:T(4,128)S(1)}, f32[4,128]{1,0:T(4,128)}, u32[]{:S(2)}) copy-start(f32[4,128]{1,0:T(4,128)} %log_ref.3) | copy-start | bytes 6148
  120.5 41.2 %copy-start.6 = (f32[4,128]{1,0:T(4,128)S(1)}, f32[4,128]{1,0:T(4,128)}, u32[]{:S(2)}) copy-start(f32[4,128]{1,0:T(4,128)} %base_ref.3) | copy-start | bytes 6148
  150.2 11.5 %collective-permute-start.3 = (f32[16,640]{1,0:T(8,128)S(1)}, f32[16,640]{1,0:T(8,128)S(1)}, u32[]{:S(2)}, u32[]{:S(2)}) collective-permute-start(f32[16,640]{1,0:T(8,128)S(1)} %get-tuple-element.21), channel_id=1, source_target_pairs={{0,16},{16,0},{1,17},{17,1},{2,18},{18,2},{3,19},{19,3},{4,20},{20... | collective-permute-start | bytes 122888 | tf_op jit(solution)/shard_map/ppermute | solution.py:218

commit v3 on v2

--- a/solution.py
+++ b/solution.py
@@ -16,7 +16,7 @@
 BF16 = jnp.bfloat16
 HIGHEST = lax.Precision.HIGHEST
 VMEM = pl.BlockSpec(memory_space=pltpu.VMEM)
-SMEM = pl.BlockSpec(memory_space=pltpu.SMEM)
+HBM = pl.BlockSpec(memory_space=pltpu.HBM)
 
 GRANT = 12 * 2**20
 
@@ -34,16 +34,16 @@
     return lax.dot_general(a, b, (((1,), (1,)), ((), ())), precision=precision, preferred_element_type=F32)
 
 
-def call(kernel, outs, arrays, scratch=(), scalars=(), cost=None):
+def call(kernel, outs, arrays, scratch=(), remote=(), cost=None):
     return pl.pallas_call(
         kernel,
         out_shape=[jax.ShapeDtypeStruct(shape, dtype) for shape, dtype in outs],
-        in_specs=[SMEM] * len(scalars) + [VMEM] * len(arrays),
+        in_specs=[HBM] * len(remote) + [VMEM] * len(arrays),
         out_specs=[VMEM] * len(outs),
         scratch_shapes=list(scratch),
         cost_estimate=cost,
         compiler_params=pltpu.CompilerParams(vmem_limit_bytes=GRANT),
-    )(*scalars, *arrays)
+    )(*(pltpu.with_memory_space_constraint(array, pltpu.HBM) for array in remote), *arrays)
 
 
 def cross_index():
@@ -54,20 +54,52 @@
     return pl.ds(pl.multiple_of(core * rows, rows), rows)
 
 
-def first_state(inverse_ref, log_ref, base_ref, direction_ref, g_ref, first_ref, second_ref):
-    core = lax.axis_index("k")
+def fetch(pairs, sems):
+    copies = [pltpu.make_async_copy(source, target, sems.at[n]) for n, (source, target) in enumerate(pairs)]
+    for copy in copies:
+        copy.start()
+    return copies
+
+
+def first_state(inverse_hbm, log_hbm, base_hbm, direction_hbm, g_ref, sent_ref, inverse_ref, log_ref, base_ref, direction_ref, sems):
+    copies = fetch(
+        [(log_hbm, log_ref), (base_hbm, base_ref), (direction_hbm, direction_ref)]
+        + [(inverse_hbm.at[q], inverse_ref.at[q]) for q in range(4)],
+        sems,
+    )
+    core = lax.axis_index("k")
+    for copy in copies[:3]:
+        copy.wait()
     alpha_u = jnp.exp(log_ref[...]) * base_ref[...]
     for q in range(4):
         forcing = -alpha_u[q][None, :] * direction_ref[:, q, :]
+        copies[3 + q].wait()
         g_ref[:, q * 128 : (q + 1) * 128] = matmul_t(forcing, inverse_ref[q], HIGHEST)
-    first_ref[...] = g_ref[of_core(core), :].astype(BF16)
-    second_ref[...] = g_ref[of_core(1 - core), :].astype(BF16)
-
-
-def build(columns_ref, counts_ref, blocks_ref, inverse_ref, weight_ref, rows_ref, noise_ref, g_ref, out_ref, seen_ref, dense):
-    core = lax.axis_index("k")
+    sent_ref[...] = g_ref[of_core(1 - core), :]
+
+
+def low_state(g_ref, came_ref, out_ref):
+    core = lax.axis_index("k")
+    out_ref[:, of_core(core, 512)] = g_ref[of_core(core), :].astype(BF16)
+    out_ref[:, of_core(1 - core, 512)] = came_ref[...].astype(BF16)
+
+
+def build(
+    columns_hbm, counts_hbm, blocks_hbm, inverse_hbm, weight_hbm, rows_hbm, noise_hbm, g_ref, after_ref, out_ref, seen_ref,
+    dense, columns_ref, counts_ref, blocks_ref, inverse_ref, weight_ref, rows_ref, noise_ref, sems,
+):
+    copies = fetch(
+        [(columns_hbm, columns_ref), (counts_hbm, counts_ref), (weight_hbm, weight_ref), (rows_hbm, rows_ref), (noise_hbm, noise_ref)]
+        + [(blocks_hbm.at[q], blocks_ref.at[q]) for q in range(4)]
+        + [(inverse_hbm.at[q], inverse_ref.at[q]) for q in range(4)],
+        sems,
+    )
+    core = lax.axis_index("k")
+    for copy in copies[:5]:
+        copy.wait()
     for q in range(4):
         dense[...] = jnp.zeros(dense.shape, F32)
+        copies[5 + q].wait()
 
         def add(slot, carry):
             lanes = pl.ds(pl.multiple_of(columns_ref[q, slot] * 128, 128), 128)
@@ -76,6 +108,7 @@
 
         lax.fori_loop(0, counts_ref[q], add, 0)
         high, low = split(dense[...])
+        copies[9 + q].wait()
         inverse, inverse_low = split(inverse_ref[q])
         out_ref[q * 128 : (q + 1) * 128, :] = (
             matmul(inverse, high) + matmul(inverse, low) + matmul(inverse_low, high)
@@ -90,7 +123,7 @@
     for q in range(4):
         seen += jnp.where(rows == q, matmul_t(g_ref[:, q * 128 : (q + 1) * 128], weight, HIGHEST), 0.0)
     seen_ref[...] = seen
-    out_ref[640:656, 512:1024], out_ref[656:672, 512:1024] = split(g_ref[of_core(1 - core), :])
+    out_ref[640:672, 512:1024] = jnp.zeros((32, 512), BF16)
     out_ref[672:688, 512:640], out_ref[672:688, 640:768] = split(seen_ref[of_core(1 - core), :])
     out_ref[672:688, 768:896], out_ref[672:688, 896:1024] = split(jnp.broadcast_to(noise_ref[...], (16, 128)))
     out_ref[688:768, 512:1024] = jnp.zeros((80, 512), BF16)
@@ -109,15 +142,12 @@
                 out_ref[share * 4 + copy if near else copy * 16 + share] = tile
 
 
-def forward_one(first_ref, second_ref, own_ref, other_ref, g_ref, out_ref, state):
-    core = lax.axis_index("k")
-    state[:, of_core(core, 512)] = first_ref[...]
-    state[:, of_core(1 - core, 512)] = second_ref[...]
-    low = state[...]
+def forward_one(low_ref, own_ref, other_ref, g_ref, came_ref, out_ref):
+    core = lax.axis_index("k")
+    low = low_ref[...]
     g_mine = g_ref[of_core(core), :]
-    g_other = joined(other_ref, slice(640, 656), slice(512, 1024), slice(656, 672), slice(512, 1024))
     put_tiles(out_ref, g_mine * (1.0 / 16) - matmul_t(low, own_ref[0:512, :]), core * 4, True)
-    put_tiles(out_ref, g_other * (1.0 / 16) - matmul_t(low, other_ref[0:512, :]), (1 - core) * 4, True)
+    put_tiles(out_ref, came_ref[...] * (1.0 / 16) - matmul_t(low, other_ref[0:512, :]), (1 - core) * 4, True)
 
 
 def sum_near(in_ref, out_ref):
@@ -201,7 +231,7 @@
             out_ref[of_core(part), q, :] = -alpha_u[q][None, :] * adjoint
 
 
-def transposed(flip):
+def transposed():
     pairs = []
     for zh in range(4):
         for cross in range(4):
@@ -209,7 +239,7 @@
                 for l in range(4):
                     for x in range(4):
                         source = (((zh * 4 + cross) * 2 + k) * 4 + l) * 4 + x
-                        target = (((l * 4 + x) * 2 + (k ^ flip)) * 4 + zh) * 4 + cross
+                        target = (((l * 4 + x) * 2 + k) * 4 + zh) * 4 + cross
                         pairs.append((source, target))
     return pairs
 
@@ -222,32 +252,44 @@
     return lax.all_to_all(array, axes, split_axis=0, concat_axis=0, tiled=True)
 
 
-def per_device(
+def apply(
     blocks, columns, counts, inverse_diag, log_inverse_permeability, base_velocity, direction, obs_rows, obs_weight, noise_prec
 ):
     rows, noise = obs_rows.reshape(1, 128), noise_prec.reshape(1, 128)
     tiles = ((64, 8, 128), BF16)
-    low_state = [pltpu.VMEM((16, 1024), BF16)]
     full_state = [pltpu.VMEM((16, 1024), F32)]
 
-    g, first, second = call(
+    g, sent = call(
         first_state,
-        [((32, 512), F32), ((16, 512), BF16), ((16, 512), BF16)],
+        [((32, 512), F32), ((16, 512), F32)],
+        [],
+        [pltpu.VMEM(shape, F32) for shape in ((4, 128, 128), (4, 128), (4, 128), (32, 4, 128))] + [pltpu.SemaphoreType.DMA((7,))],
         [inverse_diag, log_inverse_permeability, base_velocity, direction],
     )
-    first = lax.ppermute(first, AXES, transposed(0))
-    second = lax.ppermute(second, AXES, transposed(1))
+    came = swapped(sent)
+    (low,) = call(low_state, [((16, 1024), BF16)], [g, came])
+    turned = lax.ppermute(low, AXES, transposed())
     own, seen = call(
         build,
         [((768, 1024), BF16), ((32, 128), F32)],
-        [blocks, inverse_diag, obs_weight, rows, noise, g],
-        [pltpu.VMEM((128, 1024), F32)],
-        [columns, counts.reshape(4)],
+        [g, low],
+        [
+            pltpu.VMEM((128, 1024), F32),
+            pltpu.SMEM((4, 12), jnp.int32),
+            pltpu.SMEM((4,), jnp.int32),
+            pltpu.VMEM((4, 12, 128, 128), BF16),
+            pltpu.VMEM((4, 128, 128), F32),
+            pltpu.VMEM((128, 128), F32),
+            pltpu.VMEM((1, 128), jnp.int32),
+            pltpu.VMEM((1, 128), F32),
+            pltpu.SemaphoreType.DMA((13,)),
+        ],
+        [columns, counts.reshape(4), blocks, inverse_diag, obs_weight, rows, noise],
         pl.CostEstimate(flops=2 * 10**9, bytes_accessed=4 * 10**6, transcendentals=0),
     )
     other = swapped(own)
 
-    (part,) = call(forward_one, [tiles], [first, second, own, other, g], low_state)
+    (part,) = call(forward_one, [tiles], [turned, own, other, g, came])
     (part,) = call(sum_near, [tiles], [exchange(part, NEAR)])
     (part,) = call(forward_two, [((16, 16, 256), BF16)], [exchange(part, FAR), own, other, seen], full_state)
     part, predicted, force = call(
@@ -273,7 +315,7 @@
 def solution(mesh):
     grid = Mesh(mesh.devices.reshape(SIZES), AXES)
     return jax.shard_map(
-        per_device,
+        apply,
         mesh=grid,
         in_specs=(
             P(ROW, COL, None, None),

time: 164 us -> 160 us (0.976)
  local copies, waits for them, and re-layouts: 8.08 us -> 0.01 us
  Pallas kernels: 6.75 us -> 9.37 us
  waiting for transfers between devices: 1.99 us -> 4.02 us
    unnamed x26 -> x8, local copies, waits for them, and re-layouts: 8.08 us -> 0.01 us
    ppermute x2 -> x3, starting transfers between devices: 19.4 us -> 23 us  [swapped(): return lax.ppermute(array, 'k', [(0, 1), (1, 0)])]
    ppermute x2 -> x3, waiting for transfers between devices: 0.85 us -> 4.02 us  [swapped(): return lax.ppermute(array, 'k', [(0, 1), (1, 0)])]
    pallas_call x11 -> x12, Pallas kernels: 6.75 us -> 9.37 us  [call(): pl.pallas_call(kernel, out_shape=[jax.ShapeDtypeStruct(shape, dtype) for...]
    ppermute x2 -> x1, starting transfers between devices: 2.58 us -> 0.66 us  [apply(): turned = lax.ppermute(low, AXES, transposed())]
    all_to_all x7, blocking collectives: 123 us -> 122 us  [exchange(): return lax.all_to_all(array, axes, split_axis=0, concat_axis=0, tiled=True)]
  transfers between devices with their start and end apart: 4 -> 4, of which waited for: 2 -> 3; matrix products, arithmetic and copies ran while one was open for 0% -> 0% of each run, Pallas kernels for 0% -> 0%
where the time goes in v3:
time: 160 us; the launch traced here: 159 us
  blocking collectives  122 us (76%)
  starting transfers between devices  23.6 us (15%)
  Pallas kernels  9.37 us (6%)
  waiting for transfers between devices  4.02 us (3%)
    all_to_all x7, blocking collectives, exchange(): return lax.all_to_all(array, axes, split_axis=0, concat_axis=0, tiled=True)  122 us
    ppermute x3, starting transfers between devices, swapped(): return lax.ppermute(array, 'k', [(0, 1), (1, 0)])  23 us
    pallas_call x12, Pallas kernels, call(): pl.pallas_call(kernel, out_shape=[jax.ShapeDtypeStruct(shape, dtype) for...  9.37 us
    ppermute x3, waiting for transfers between devices, swapped(): return lax.ppermute(array, 'k', [(0, 1), (1, 0)])  4.02 us
  transfers between devices with their start and end apart: 4, of which 3 were waited for; matrix products, arithmetic and copies ran while one was open for 0% of the time, Pallas kernels for 0%

profile of v3, /device:TPU:1, one launch (start us, length us, event | category | flops | bytes accessed | tf_op | source)
XLA Modules:
  0.0 159.4 jit_solution(18433605227459916843)
XLA Ops:
  0.6 2.3 %shard_map.113 = (f32[32,512]{1,0:T(8,128)S(1)}, f32[16,512]{1,0:T(8,128)S(1)}) custom-call(f32[4,128,128]{2,1,0:T(8,128)} %inverse_ref.1, f32[4,128]{1,0:T(4,128)} %log_ref.1, f32[4,128]{1,0:T(4,128)} %base_ref.1, f32[32,4,128]{2,1,0:T(4,128)} %direction_hbm.1), custom_call_target="tpu_custom_call" | custom-call | tf_op jit(solution)/shard_map/pallas_call | solution.py:38
  2.9 8.7 %collective-permute-start = (f32[16,512]{1,0:T(8,128)S(1)}, f32[16,512]{1,0:T(8,128)S(1)}, u32[]{:S(2)}, u32[]{:S(2)}) collective-permute-start(f32[16,512]{1,0:T(8,128)S(1)} %get-tuple-element.12), channel_id=1, source_target_pairs={{0,16},{16,0},{1,17},{17,1},{2,18},{18,2},{3,19},{19,3},{4,20},{20... | collective-permute-start | bytes 98312 | tf_op jit(solution)/shard_map/ppermute | solution.py:248
  11.7 0.8 collective-permute-done.came_ref
  12.5 4.3 %shard_map.115 = (bf16[768,1024]{1,0:T(8,128)(2,1)S(1)}, f32[32,128]{1,0:T(8,128)S(1)}) custom-call(s32[4,12]{1,0:T(4,128)} %columns_hbm.1, s32[4]{0:T(128)} %bitcast.5, bf16[4,12,128,128]{3,2,1,0:T(8,128)(2,1)} %blocks_hbm.1, f32[4,128,128]{2,1,0:T(8,128)} %inverse_ref.1, f32[128,128]{1,0:T(8,128)} %weight_hbm.1, s32[1,128]{1,0:T(1,128)} %bitcast.6, ...), custom_call_target="tpu_custom_call" | custom-call | flops 2000000000 | bytes 4000000 | tf_op jit(solution)/shard_map/pallas_call | solution.py:38
  16.8 2.4 %collective-permute-start.2 = (bf16[768,1024]{1,0:T(8,128)(2,1)S(1)}, bf16[768,1024]{1,0:T(8,128)(2,1)S(1)}, u32[]{:S(2)}, u32[]{:S(2)}) collective-permute-start(bf16[768,1024]{1,0:T(8,128)(2,1)S(1)} %get-tuple-element.13.own_ref), channel_id=1, source_target_pairs={{0,16},{16,0},{1,17},{17,1},{2,18},{18,2},{3,19},{19,3},{4,20},{20... | collective-permute-start | bytes 4718600 | tf_op jit(solution)/shard_map/ppermute | solution.py:248
  19.2 0.7 collective-permute-start.1
  19.9 0.0 collective-permute-done.1.low_ref
  19.9 2.3 %collective-permute-done.2.other_ref = bf16[768,1024]{1,0:T(8,128)(2,1)S(1)} collective-permute-done((bf16[768,1024]{1,0:T(8,128)(2,1)S(1)}, bf16[768,1024]{1,0:T(8,128)(2,1)S(1)}, u32[]{:S(2)}, u32[]{:S(2)}) %collective-permute-start.2) | collective-permute-done | bytes 1572896 | tf_op jit(solution)/shard_map/ppermute | solution.py:248
  22.2 0.7 shard_map.116
  22.9 26.4 %all_to_all.35.in_ref = bf16[64,8,128]{2,1,0:T(8,128)(2,1)S(1)} all-to-all(bf16[64,8,128]{2,1,0:T(8,128)(2,1)S(1)} %shard_map.116), channel_id=1, replica_groups=mesh['zh'=4,'z0'=2,'h'=2,'k'=2,'l'=4,'x'=4] {'z0','h','l','x'}, dimensions={0} | all-to-all | bytes 262144 | tf_op jit(solution)/shard_map/all_to_all | solution.py:252
  49.3 24.6 %all_to_all.36.in_ref = bf16[64,8,128]{2,1,0:T(8,128)(2,1)S(1)} all-to-all(bf16[64,8,128]{2,1,0:T(8,128)(2,1)S(1)} %shard_map.117), channel_id=1, replica_groups=mesh['zh'=4,'z0'=2,'h'=2,'k'=2,'l'=4,'x'=4] {'zh','z0','h','l'}, dimensions={0} | all-to-all | bytes 262144 | tf_op jit(solution)/shard_map/all_to_all | solution.py:252
  74.0 0.0 copy-start.3
  74.0 0.3 shard_map.118
  74.2 10.8 %all_to_all.37.in_ref = bf16[16,16,256]{2,1,0:T(8,128)(2,1)S(1)} all-to-all(bf16[16,16,256]{2,1,0:T(8,128)(2,1)S(1)} %shard_map.118), channel_id=1, replica_groups=mesh['zh'=4,'z0'=2,'h'=2,'k'=2,'l'=4,'x'=4] {'l','x'}, dimensions={0} | all-to-all | bytes 262144 | tf_op jit(solution)/shard_map/all_to_all | solution.py:252
  85.1 0.0 copy-done.3
  85.1 0.2 shard_map.119
  85.3 16.7 %all_to_all.38.in_ref = bf16[64,8,128]{2,1,0:T(8,128)(2,1)S(1)} all-to-all(bf16[64,8,128]{2,1,0:T(8,128)(2,1)S(1)} %get-tuple-element.15), channel_id=1, replica_groups=mesh['zh'=4,'z0'=2,'h'=2,'k'=2,'l'=4,'x'=4] {'zh','z0','h','l'}, dimensions={0} | all-to-all | bytes 262144 | tf_op jit(solution)/shard_map/all_to_all | solution.py:252
  102.0 13.8 %all_to_all.39.in_ref = bf16[64,8,128]{2,1,0:T(8,128)(2,1)S(1)} all-to-all(bf16[64,8,128]{2,1,0:T(8,128)(2,1)S(1)} %shard_map.120), channel_id=1, replica_groups=mesh['zh'=4,'z0'=2,'h'=2,'k'=2,'l'=4,'x'=4] {'z0','h','l','x'}, dimensions={0} | all-to-all | bytes 262144 | tf_op jit(solution)/shard_map/all_to_all | solution.py:252
  115.8 0.0 copy-start
  115.8 0.0 copy-start.1
  115.8 0.0 copy-start.2
  115.8 0.4 shard_map.121
  116.2 15.3 %all_to_all.40.in_ref = bf16[64,8,128]{2,1,0:T(8,128)(2,1)S(1)} all-to-all(bf16[64,8,128]{2,1,0:T(8,128)(2,1)S(1)} %shard_map.121), channel_id=1, replica_groups=mesh['zh'=4,'z0'=2,'h'=2,'k'=2,'l'=4,'x'=4] {'zh','z0','h','l'}, dimensions={0} | all-to-all | bytes 262144 | tf_op jit(solution)/shard_map/all_to_all | solution.py:252
  131.5 14.0 %all_to_all.41.in_ref = bf16[64,8,128]{2,1,0:T(8,128)(2,1)S(1)} all-to-all(bf16[64,8,128]{2,1,0:T(8,128)(2,1)S(1)} %shard_map.122), channel_id=1, replica_groups=mesh['zh'=4,'z0'=2,'h'=2,'k'=2,'l'=4,'x'=4] {'z0','h','l','x'}, dimensions={0} | all-to-all | bytes 262144 | tf_op jit(solution)/shard_map/all_to_all | solution.py:252
  145.5 11.8 %collective-permute-start.3 = (f32[16,640]{1,0:T(8,128)S(1)}, f32[16,640]{1,0:T(8,128)S(1)}, u32[]{:S(2)}, u32[]{:S(2)}) collective-permute-start(f32[16,640]{1,0:T(8,128)S(1)} %get-tuple-element.19), channel_id=1, source_target_pairs={{0,16},{16,0},{1,17},{17,1},{2,18},{18,2},{3,19},{19,3},{4,20},{20... | collective-permute-start | bytes 122888 | tf_op jit(solution)/shard_map/ppermute | solution.py:248
  157.4 0.8 collective-permute-done.3.came_ref
  158.2 0.0 copy-done
  158.2 0.0 copy-done.1
  158.2 0.0 copy-done.2
  158.2 1.2 shard_map.124
  (5 shorter events, 0.1 us)
Async XLA Ops:
  2.9 9.6 %collective-permute-start = (f32[16,512]{1,0:T(8,128)S(1)}, f32[16,512]{1,0:T(8,128)S(1)}, u32[]{:S(2)}, u32[]{:S(2)}) collective-permute-start(f32[16,512]{1,0:T(8,128)S(1)} %get-tuple-element.12), channel_id=1, source_target_pairs={{0,16},{16,0},{1,17},{17,1},{2,18},{18,2},{3,19},{19,3},{4,20},{20... | collective-permute-start | bytes 98312 | tf_op jit(solution)/shard_map/ppermute | solution.py:248
  16.8 5.4 %collective-permute-start.2 = (bf16[768,1024]{1,0:T(8,128)(2,1)S(1)}, bf16[768,1024]{1,0:T(8,128)(2,1)S(1)}, u32[]{:S(2)}, u32[]{:S(2)}) collective-permute-start(bf16[768,1024]{1,0:T(8,128)(2,1)S(1)} %get-tuple-element.13.own_ref), channel_id=1, source_target_pairs={{0,16},{16,0},{1,17},{17,1},{2,18},{18,2},{3,19},{19,3},{4,20},{20... | collective-permute-start | bytes 4718600 | tf_op jit(solution)/shard_map/ppermute | solution.py:248
  19.2 0.7 collective-permute-start.1
  74.0 11.1 %copy-start.3 = (f32[128]{0:T(128)S(1)}, f32[128]{0:T(128)}, u32[]{:S(2)}) copy-start(f32[128]{0:T(128)} %param.19) | copy-start | bytes 1540
  115.8 42.5 %copy-start = (f32[4,128,128]{2,1,0:T(8,128)S(1)}, f32[4,128,128]{2,1,0:T(8,128)}, u32[]{:S(2)}) copy-start(f32[4,128,128]{2,1,0:T(8,128)} %inverse_ref.1) | copy-start | bytes 786436
  115.8 42.5 %copy-start.1 = (f32[4,128]{1,0:T(4,128)S(1)}, f32[4,128]{1,0:T(4,128)}, u32[]{:S(2)}) copy-start(f32[4,128]{1,0:T(4,128)} %log_ref.1) | copy-start | bytes 6148
  115.8 42.5 %copy-start.2 = (f32[4,128]{1,0:T(4,128)S(1)}, f32[4,128]{1,0:T(4,128)}, u32[]{:S(2)}) copy-start(f32[4,128]{1,0:T(4,128)} %base_ref.1) | copy-start | bytes 6148
  145.5 12.7 %collective-permute-start.3 = (f32[16,640]{1,0:T(8,128)S(1)}, f32[16,640]{1,0:T(8,128)S(1)}, u32[]{:S(2)}, u32[]{:S(2)}) collective-permute-start(f32[16,640]{1,0:T(8,128)S(1)} %get-tuple-element.19), channel_id=1, source_target_pairs={{0,16},{16,0},{1,17},{17,1},{2,18},{18,2},{3,19},{19,3},{4,20},{20... | collective-permute-start | bytes 122888 | tf_op jit(solution)/shard_map/ppermute | solution.py:248
